TPU v7x, 32 devices: a whole 2x2x4 slice. The times are simulated.
32 devices in a mesh: tile: 8 (over z, x), mem: 4 (over y, core).
Axes of the slice: x: 2, y: 2, z: 4, core: 2. Of those that a mesh axis runs over, the one named last changes fastest.
Arguments:
- prior_ensemble_fields: float32 [128, 32, 512], P('mem', 'tile'), may hold values from -6 to 6
- vel_y: float32 [32, 512], P('tile'), may hold values from -0.4 to 0.4
- vel_x: float32 [32, 512], P('tile'), may hold values from -0.4 to 0.4
- diffus: float32 [32, 512], P('tile'), may hold values from 0.02 to 0.2
- assign: int32 [8, 2048], P('tile'), may hold values from 0 to 2047, each once within a row
- obs_cell: int32 [64, 512], P(('tile', 'mem')), may hold values from 0 to 255
- obs_value: float32 [64, 512], P(('tile', 'mem')), may hold values from -6 to 6
- obs_var: float32 [64, 512], P(('tile', 'mem')), may hold values from 0.2 to 2
Outputs:
- analysis: float32 [128, 32, 512], P('mem', 'tile')
All inputs are finite; a program needn't handle non-finite values.
Results may differ from a plain program's by a relative error of at most 0.0003.
Values sent between devices are 32-bit elements; how exact they have to be, the bound alone decides.
A program may use at most 64 MiB of HBM per device.

v0:
```python
import jax
import jax.numpy as jnp
from jax import lax
from jax.sharding import PartitionSpec as P

PATCH = 256


def extended(block, sides, width):
    for axis, dim in sides:
        count = lax.axis_size(axis)
        forward = [(i, i + 1) for i in range(count - 1)]
        backward = [(target, source) for source, target in forward]
        low = lax.ppermute(
            lax.slice_in_dim(block, block.shape[dim] - width, None, axis=dim), axis, forward
        )
        high = lax.ppermute(lax.slice_in_dim(block, 0, width, axis=dim), axis, backward)
        block = jnp.concatenate([low, block, high], axis=dim)
    return block


def advance(padded, coef_y, coef_x, coef_k):
    center = padded[..., 2:-2, :]
    above = padded[..., 3:-1, :]
    below = padded[..., 1:-3, :]
    grad_y = (-padded[..., 4:, :] + 8.0 * above - 8.0 * below + padded[..., :-4, :]) / 12.0
    lap_y = above - 2.0 * center + below
    right_one = jnp.roll(center, -1, axis=-1)
    left_one = jnp.roll(center, 1, axis=-1)
    grad_x = (
        -jnp.roll(center, -2, axis=-1)
        + 8.0 * right_one
        - 8.0 * left_one
        + jnp.roll(center, 2, axis=-1)
    ) / 12.0
    lap_x = right_one - 2.0 * center + left_one
    return center - coef_y * grad_y - coef_x * grad_x + coef_k * (lap_y + lap_x)


def analyze(members, cells, observed, variance):
    ensemble_size = members.shape[0]
    highest = lax.Precision.HIGHEST
    center = jnp.mean(members, axis=0)
    spread = members - center[None, :]
    obs_spread = jnp.take(spread, cells, axis=1)
    innovation = observed - jnp.take(center, cells)
    weighted = obs_spread / variance[None, :]
    gram = jnp.dot(weighted, obs_spread.T, precision=highest, preferred_element_type=jnp.float32)
    system = gram + (ensemble_size - 1.0) * jnp.eye(ensemble_size, dtype=jnp.float32)
    factor = jnp.linalg.cholesky(system)
    pulled = jnp.dot(weighted, innovation, precision=highest, preferred_element_type=jnp.float32)
    right_side = jnp.concatenate([pulled[:, None], gram], axis=1)
    solved = jax.scipy.linalg.cho_solve((factor, True), right_side)
    gain_mean = solved[:, 0]
    mixing = solved[:, 1:]
    transform = jnp.eye(ensemble_size, dtype=jnp.float32) - 0.5 * mixing + gain_mean[None, :]
    return center[None, :] + jnp.dot(
        transform, spread, precision=highest, preferred_element_type=jnp.float32
    )


def on_device(prior_ensemble_fields, vel_y, vel_x, diffus, assign, obs_cell, obs_value, obs_var):
    local_members, tile_rows, width_cells = prior_ensemble_fields.shape
    columns = tile_rows * width_cells
    groups = lax.axis_size("mem")
    group_columns = columns // groups
    patches_here = group_columns // PATCH
    ensemble = prior_ensemble_fields
    stacked = jnp.concatenate([ensemble, vel_y[None], vel_x[None], diffus[None]], axis=0)
    widened = extended(stacked, (("tile", 1),), 4)
    field_rows = widened[:local_members]
    near_y = widened[local_members, 2:-2]
    near_x = widened[local_members + 1, 2:-2]
    near_k = widened[local_members + 2, 2:-2]
    middle = advance(field_rows, near_y, near_x, near_k)
    first_row = lax.axis_index("tile") * tile_rows - 2
    global_rows = first_row + jnp.arange(tile_rows + 4, dtype=jnp.int32)
    inside = (global_rows >= 0) & (global_rows < tile_rows * lax.axis_size("tile"))
    middle = jnp.where(inside[None, :, None], middle, 0.0)
    ensemble = advance(middle, vel_y, vel_x, diffus)
    order = assign[0]
    permuted = jnp.take(ensemble.reshape(local_members, columns), order, axis=1)
    blocks = permuted.reshape(local_members, groups, group_columns)
    gathered = lax.all_to_all(blocks, "mem", split_axis=1, concat_axis=0, tiled=True)
    gathered = gathered.reshape(local_members * groups, patches_here, PATCH)
    updated = jax.vmap(analyze, in_axes=(1, 0, 0, 0), out_axes=1)(
        gathered, obs_cell, obs_value, obs_var
    )
    outgoing = updated.reshape(local_members * groups, 1, group_columns)
    returned = lax.all_to_all(outgoing, "mem", split_axis=0, concat_axis=1, tiled=True)
    returned = returned.reshape(local_members, columns)
    positions = jnp.argsort(order)
    analysed = jnp.take(returned, positions, axis=1).reshape(local_members, tile_rows, width_cells)
    padded = extended(analysed, (("tile", 1),), 2)
    return advance(padded, vel_y, vel_x, diffus)


def solution(mesh):
    return jax.shard_map(
        on_device,
        mesh=mesh,
        in_specs=(
            P("mem", "tile", None),
            P("tile", None),
            P("tile", None),
            P("tile", None),
            P("tile", None),
            P(("tile", "mem"), None),
            P(("tile", "mem"), None),
            P(("tile", "mem"), None),
        ),
        out_specs=P("mem", "tile", None),
        check_vma=False,
    )
```

profile of v0, /device:TPU:16, one launch (start us, length us, event | category | flops | bytes accessed | tf_op | source)
XLA Modules:
  0.0 133.3 jit_solution(381985108282282040)
XLA Ops:
  0.0 1.1 pad_maximum_fusion.11
  1.1 3.4 %collective-permute-start = (f32[35,4,512]{2,1,0:T(4,128)S(1)}, f32[35,4,512]{2,1,0:T(4,128)S(1)}, u32[]{:S(2)}, u32[]{:S(2)}) collective-permute-start(f32[35,4,512]{2,1,0:T(4,128)S(1)} %pad_maximum_fusion.11), channel_id=1, source_target_pairs={{0,4},{4,8},{8,12},{12,16},{16,20},{20,24},{24,28},{1,5},{5,9},{9,... | collective-permute-start | bytes 860168 | tf_op jit(solution)/shard_map/ppermute | solution.py:14
  4.5 3.3 %collective-permute-start.1 = (f32[35,4,512]{2,1,0:T(4,128)S(1)}, f32[35,4,512]{2,1,0:T(4,128)S(1)}, u32[]{:S(2)}, u32[]{:S(2)}) collective-permute-start(f32[35,4,512]{2,1,0:T(4,128)S(1)} %pad_maximum_fusion.11), channel_id=1, source_target_pairs={{4,0},{8,4},{12,8},{16,12},{20,16},{24,20},{28,24},{5,1},{9,5},{13... | collective-permute-start | bytes 860168 | tf_op jit(solution)/shard_map/ppermute | solution.py:17
  7.8 0.7 fusion.66
  8.5 0.7 compare_and_fusion.1
  9.3 0.7 fusion.68
  10.0 5.7 %sort.17 = (s32[2048]{0:T(1024)}, s32[2048]{0:T(1024)S(1)}) sort(s32[2048]{0:T(1024)} %bitcast.89, s32[2048]{0:T(1024)S(1)} %iota.82), dimensions={0}, to_apply=%region_3.5 | sort | flops 22528 | bytes 32768 | tf_op jit(solution)/shard_map/jit(argsort)/sort | solution.py:92
  15.8 0.7 broadcast_multiply_fusion
  16.5 0.2 collective-permute-done
  16.7 1.9 %collective-permute-done.1 = f32[35,4,512]{2,1,0:T(4,128)S(1)} collective-permute-done((f32[35,4,512]{2,1,0:T(4,128)S(1)}, f32[35,4,512]{2,1,0:T(4,128)S(1)}, u32[]{:S(2)}, u32[]{:S(2)}) %collective-permute-start.1) | collective-permute-done | bytes 286752 | tf_op jit(solution)/shard_map/ppermute | solution.py:17
  18.6 1.2 pad_maximum_fusion
  19.8 0.3 fusion.74
  20.1 0.3 fusion.77
  20.6 0.4 copy-done
  21.1 0.9 fusion.6
  21.9 0.2 fusion.78
  22.1 0.2 fusion.81
  22.6 0.8 fusion.29
  23.4 0.3 copy.81
  23.7 5.5 %gather_fusion.2 = f32[2048,32]{1,0:T(8,128)S(1)} fusion(f32[32,2048]{0,1:T(8,128)S(1)} %bitcast.66, s32[2048]{0:T(1024)S(1)} %fusion.66), kind=kCustom, calls=%fused_computation.clone | custom fusion | bytes 532480 | tf_op jit(solution)/shard_map/jit(_take)/gather | solution.py:82
  29.2 0.3 broadcast_select_fusion.1
  29.6 1.0 copy.82
  30.6 3.6 %all-to-all-start = ((f32[32,4,512]{2,0,1:T(8,128)}), f32[32,4,512]{2,0,1:T(8,128)S(1)}, u32[]{:S(2)}, u32[]{:S(2)}) async-start(f32[32,4,512]{2,0,1:T(8,128)} %copy.82), calls=%async_computation | async-start | bytes 524288 | tf_op jit(solution)/shard_map/all_to_all | solution.py:84
  34.2 5.8 %all-to-all-done = f32[32,4,512]{2,0,1:T(8,128)S(1)} async-done(((f32[32,4,512]{2,0,1:T(8,128)}), f32[32,4,512]{2,0,1:T(8,128)S(1)}, u32[]{:S(2)}, u32[]{:S(2)}) %all-to-all-start) | async-done | bytes 262176 | tf_op jit(solution)/shard_map/all_to_all | solution.py:84
  40.0 0.2 reshape.84
  40.5 9.1 %gather_fusion.1 = f32[1024]{0:T(1024)S(1)} fusion(f32[2,256]{1,0:T(2,128)S(1)} %div.32, s32[1024]{0:T(1024)S(1)} %bitcast.64), kind=kCustom, calls=%fused_computation.3 | custom fusion | bytes 16384 | tf_op jit(solution)/shard_map/vmap(jit(_take))/gather | solution.py:46
  49.6 6.8 %gather_fusion = f32[1024,128]{1,0:T(8,128)S(1)} fusion(f32[2,128,256]{1,2,0:T(8,128)S(1)} %subtract_bitcast_fusion, s32[1024]{0:T(1024)S(1)} %bitcast.65), kind=kCustom, calls=%fused_computation.2 | custom fusion | bytes 1056768 | tf_op jit(solution)/shard_map/vmap(jit(_take))/gather | solution.py:45
  56.5 1.8 %fusion.14 = f32[2,128,128]{1,2,0:T(8,128)S(1)} fusion(f32[2,512,128]{2,1,0:T(8,128)S(1)} %bitcast.73, f32[2,512]{1,0:T(2,128)S(1)} %copy-done.6, pred[2,512]{1,0:T(4,128)(4,1)S(1)} %get-tuple-element.9), kind=kOutput, calls=%fused_computation.38 | convolution fusion | flops 201719808 | bytes 660480 | tf_op jit(solution)/shard_map/vmap()/dot_general | solution.py:48
  58.5 23.5 %custom-call.11 = f32[2,128,128]{2,1,0:T(8,128)S(1)} custom-call(f32[2,128,128]{2,1,0:T(8,128)S(1)} %fusion.54), custom_call_target="Cholesky" | custom-call | tf_op jit(solution)/shard_map/vmap(jit(cholesky))/cholesky | solution.py:50
  82.2 19.7 %custom-call.12 = f32[2,1,128,128]{2,3,1,0:T(8,128)S(1)} custom-call(f32[2,1,128,128]{3,2,1,0:T(8,128)S(1)} %select_bitcast_fusion), custom_call_target="InvertDiagBlocksLowerTriangular" | custom-call | tf_op jit(solution)/shard_map/vmap(jit(_cho_solve))/triangular_solve | solution.py:53
  101.9 0.6 convolution_bitcast_fusion
  102.5 0.4 fusion.46
  102.9 0.4 fusion.50
  103.4 0.5 fusion
  104.0 0.8 copy.91
  104.9 3.4 %all-to-all-start.1 = ((f32[128,1,512]{2,1,0:T(1,128)}), f32[128,1,512]{2,1,0:T(1,128)S(1)}, u32[]{:S(2)}, u32[]{:S(2)}) async-start(f32[128,1,512]{2,1,0:T(1,128)} %copy.91), calls=%async_computation.1 | async-start | bytes 524288 | tf_op jit(solution)/shard_map/all_to_all | solution.py:90
  108.3 6.0 %all-to-all-done.1 = f32[128,1,512]{2,1,0:T(1,128)S(1)} async-done(((f32[128,1,512]{2,1,0:T(1,128)}), f32[128,1,512]{2,1,0:T(1,128)S(1)}, u32[]{:S(2)}, u32[]{:S(2)}) %all-to-all-start.1) | async-done | bytes 262176 | tf_op jit(solution)/shard_map/all_to_all | solution.py:90
  114.3 0.3 copy.92
  114.6 5.5 %gather_fusion.3 = f32[2048,32]{1,0:T(8,128)S(1)} fusion(f32[32,2048]{0,1:T(8,128)S(1)} %bitcast.67, s32[2048]{0:T(1024)S(1)} %fusion.67), kind=kCustom, calls=%fused_computation.1.clone | custom fusion | bytes 532480 | tf_op jit(solution)/shard_map/jit(_take)/gather | solution.py:93
  120.1 0.3 broadcast_select_fusion
  120.4 0.3 copy.97
  120.8 0.2 fusion.82
  121.0 0.2 fusion.85
  121.4 2.4 %collective-permute-start.2 = (f32[32,2,512]{2,1,0:T(2,128)S(1)}, f32[32,2,512]{2,1,0:T(2,128)S(1)}, u32[]{:S(2)}, u32[]{:S(2)}) collective-permute-start(f32[32,2,512]{2,1,0:T(2,128)S(1)} %get-tuple-element.38), channel_id=1, source_target_pairs={{4,0},{8,4},{12,8},{16,12},{20,16},{24,20},{28,24},{5,1},{9,5},{13... | collective-permute-start | bytes 393224 | tf_op jit(solution)/shard_map/ppermute | solution.py:17
  123.8 3.5 %collective-permute-start.3 = (f32[32,2,512]{2,1,0:T(2,128)S(1)}, f32[32,2,512]{2,1,0:T(2,128)S(1)}, u32[]{:S(2)}, u32[]{:S(2)}) collective-permute-start(f32[32,2,512]{2,1,0:T(2,128)S(1)} %get-tuple-element.37), channel_id=1, source_target_pairs={{0,4},{4,8},{8,12},{12,16},{16,20},{20,24},{24,28},{1,5},{5,9},{9,... | collective-permute-start | bytes 393224 | tf_op jit(solution)/shard_map/ppermute | solution.py:14
  127.3 0.9 collective-permute-done.2
  128.2 3.3 %collective-permute-done.3 = f32[32,2,512]{2,1,0:T(2,128)S(1)} collective-permute-done((f32[32,2,512]{2,1,0:T(2,128)S(1)}, f32[32,2,512]{2,1,0:T(2,128)S(1)}, u32[]{:S(2)}, u32[]{:S(2)}) %collective-permute-start.3) | collective-permute-done | bytes 131104 | tf_op jit(solution)/shard_map/ppermute | solution.py:14
  131.5 1.7 %fusion.25 = f32[32,4,512]{2,1,0:T(4,128)} fusion(f32[32,4,512]{2,1,0:T(4,128)S(1)} %copy.97, f32[32,2,512]{2,1,0:T(2,128)S(1)} %collective-permute-done.2, f32[32,2,512]{2,1,0:T(2,128)S(1)} %collective-permute-done.3, f32[32,4,2]{2,1,0:T(4,128)S(1)} %get-tuple-element.34, f32[32,4,510]{2,1,0:T(4,128)S(1)} %get-tuple-element.36, ...), kind=kLoop, calls=%fused_computation.51 | loop fusion | flops 2097152 | bytes 1859584 | tf_op jit(solution)/shard_map/add | solution.py:37
  (47 shorter events, 1.8 us)
Async XLA Ops:
  1.1 15.6 %collective-permute-start = (f32[35,4,512]{2,1,0:T(4,128)S(1)}, f32[35,4,512]{2,1,0:T(4,128)S(1)}, u32[]{:S(2)}, u32[]{:S(2)}) collective-permute-start(f32[35,4,512]{2,1,0:T(4,128)S(1)} %pad_maximum_fusion.11), channel_id=1, source_target_pairs={{0,4},{4,8},{8,12},{12,16},{16,20},{20,24},{24,28},{1,5},{5,9},{9,... | collective-permute-start | bytes 860168 | tf_op jit(solution)/shard_map/ppermute | solution.py:14
  4.5 14.1 %collective-permute-start.1 = (f32[35,4,512]{2,1,0:T(4,128)S(1)}, f32[35,4,512]{2,1,0:T(4,128)S(1)}, u32[]{:S(2)}, u32[]{:S(2)}) collective-permute-start(f32[35,4,512]{2,1,0:T(4,128)S(1)} %pad_maximum_fusion.11), channel_id=1, source_target_pairs={{4,0},{8,4},{12,8},{16,12},{20,16},{24,20},{28,24},{5,1},{9,5},{13... | collective-permute-start | bytes 860168 | tf_op jit(solution)/shard_map/ppermute | solution.py:17
  20.1 1.0 copy-start
  20.1 0.9 copy-start.1
  20.1 0.9 copy-start.2
  20.1 0.9 copy-start.3
  30.6 9.4 %all-to-all-start = ((f32[32,4,512]{2,0,1:T(8,128)}), f32[32,4,512]{2,0,1:T(8,128)S(1)}, u32[]{:S(2)}, u32[]{:S(2)}) async-start(f32[32,4,512]{2,0,1:T(8,128)} %copy.82), calls=%async_computation | async-start | bytes 524288 | tf_op jit(solution)/shard_map/all_to_all | solution.py:84
  49.6 6.8 %copy-start.4 = (s32[2,512]{1,0:T(2,128)S(1)}, s32[2,512]{1,0:T(2,128)}, u32[]{:S(2)}) copy-start(s32[2,512]{1,0:T(2,128)} %param.15) | copy-start | bytes 12292
  49.6 6.8 %copy-start.5 = (f32[2,512]{1,0:T(2,128)S(1)}, f32[2,512]{1,0:T(2,128)}, u32[]{:S(2)}) copy-start(f32[2,512]{1,0:T(2,128)} %param.16) | copy-start | bytes 12292
  49.6 6.9 %copy-start.6 = (f32[2,512]{1,0:T(2,128)S(1)}, f32[2,512]{1,0:T(2,128)}, u32[]{:S(2)}) copy-start(f32[2,512]{1,0:T(2,128)} %param.17) | copy-start | bytes 12292
  104.9 9.4 %all-to-all-start.1 = ((f32[128,1,512]{2,1,0:T(1,128)}), f32[128,1,512]{2,1,0:T(1,128)S(1)}, u32[]{:S(2)}, u32[]{:S(2)}) async-start(f32[128,1,512]{2,1,0:T(1,128)} %copy.91), calls=%async_computation.1 | async-start | bytes 524288 | tf_op jit(solution)/shard_map/all_to_all | solution.py:90
  121.4 6.9 %collective-permute-start.2 = (f32[32,2,512]{2,1,0:T(2,128)S(1)}, f32[32,2,512]{2,1,0:T(2,128)S(1)}, u32[]{:S(2)}, u32[]{:S(2)}) collective-permute-start(f32[32,2,512]{2,1,0:T(2,128)S(1)} %get-tuple-element.38), channel_id=1, source_target_pairs={{4,0},{8,4},{12,8},{16,12},{20,16},{24,20},{28,24},{5,1},{9,5},{13... | collective-permute-start | bytes 393224 | tf_op jit(solution)/shard_map/ppermute | solution.py:17
  123.8 7.8 %collective-permute-start.3 = (f32[32,2,512]{2,1,0:T(2,128)S(1)}, f32[32,2,512]{2,1,0:T(2,128)S(1)}, u32[]{:S(2)}, u32[]{:S(2)}) collective-permute-start(f32[32,2,512]{2,1,0:T(2,128)S(1)} %get-tuple-element.37), channel_id=1, source_target_pairs={{0,4},{4,8},{8,12},{12,16},{16,20},{20,24},{24,28},{1,5},{5,9},{9,... | collective-permute-start | bytes 393224 | tf_op jit(solution)/shard_map/ppermute | solution.py:14
where the time goes:
time: 134 us; the launch traced here: 133 us
  other arithmetic  58.6 us (44%)
  local copies, waits for them, and re-layouts  32.9 us (25%)
  starting transfers between devices  19.6 us (15%)
  waiting for transfers between devices  18 us (13%)
  matrix products  3.69 us (3%)
    another operation x3, other arithmetic, analyze(): factor = jnp.linalg.cholesky(system)  23.6 us
    another operation x3, other arithmetic, analyze(): solved = jax.scipy.linalg.cho_solve((factor, True), right_side)  19.8 us
    gather x2, local copies, waits for them, and re-layouts, analyze(): innovation = observed - jnp.take(center, cells)  9.12 us
    ppermute x2, starting transfers between devices, extended(): lax.ppermute(lax.slice_in_dim(block, block.shape[dim] - width, None, axis...  6.85 us
    gather x1, local copies, waits for them, and re-layouts, analyze(): obs_spread = jnp.take(spread, cells, axis=1)  6.79 us
    all_to_all x1, waiting for transfers between devices, on_device(): lax.all_to_all(outgoing, 'mem', split_axis=0, concat_axis=1, tiled=True)  5.96 us
    all_to_all x1, waiting for transfers between devices, on_device(): lax.all_to_all(blocks, 'mem', split_axis=1, concat_axis=0, tiled=True)  5.78 us
    sort x1, other arithmetic, on_device(): positions = jnp.argsort(order)  5.74 us
  transfers between devices with their start and end apart: 6, of which 6 were waited for; matrix products, arithmetic and copies ran while one was open for 7% of the time, Pallas kernels for 0%

commit v1 on v0

--- a/solution.py
+++ b/solution.py
@@ -1,6 +1,8 @@
 import jax
 import jax.numpy as jnp
 from jax import lax
+from jax.experimental import pallas as pl
+from jax.experimental.pallas import tpu as pltpu
 from jax.sharding import PartitionSpec as P
 
 PATCH = 256
@@ -37,26 +39,92 @@
     return center - coef_y * grad_y - coef_x * grad_x + coef_k * (lap_y + lap_x)
 
 
+def dot(a, b, dims=(((1,), (0,)), ((), ()))):
+    return lax.dot_general(
+        a, b, dims, precision=lax.Precision.HIGHEST, preferred_element_type=jnp.float32
+    )
+
+
+NT = (((1,), (1,)), ((), ()))
+
+
+def analysis_kernel(members_ref, cells_ref, observed_ref, variance_ref, out_ref, system_ref, inverse_ref):
+    size = members_ref.shape[0]
+    patches = cells_ref.shape[0]
+    floor = size - 1.0
+    eye = jnp.where(
+        lax.broadcasted_iota(jnp.int32, (size, size), 0)
+        == lax.broadcasted_iota(jnp.int32, (size, size), 1),
+        1.0,
+        0.0,
+    )
+    spreads, centers, pulls, excess = [], [], [], []
+    for p in range(patches):
+        x = members_ref[:, p * PATCH : (p + 1) * PATCH]
+        center = jnp.mean(x, axis=0, keepdims=True)
+        spread = x - center
+        cells = cells_ref[p : p + 1, :]
+        nobs = cells.shape[1]
+        hot = jnp.where(
+            lax.broadcasted_iota(jnp.int32, (PATCH, nobs), 0) == cells, 1.0, 0.0
+        )
+        inverse_var = 1.0 / variance_ref[p : p + 1, :]
+        pair = jnp.concatenate(
+            [inverse_var, observed_ref[p : p + 1, :] * inverse_var, jnp.zeros((6, nobs), jnp.float32)],
+            axis=0,
+        )
+        sums = dot(pair, hot, NT)
+        d, w = sums[0:1], sums[1:2]
+        gram = dot(spread * d, spread, NT)
+        pulled = dot(jnp.broadcast_to(w - d * center, (8, PATCH)), spread, NT)
+        bound = jnp.max(jnp.sum(jnp.abs(gram), axis=0, keepdims=True)) * 1.0001
+        system = gram + floor * eye
+        system_ref[p] = system
+        scale = 2.0 / (2.0 * floor + bound)
+        inverse_ref[p] = (2.0 * scale) * eye - (scale * scale) * system
+        e = bound / floor
+        spreads.append(spread)
+        centers.append(center)
+        pulls.append(pulled)
+        excess.append(e * e / (4.0 * (1.0 + e)))
+
+    def more(es):
+        worst = es[0]
+        for e in es[1:]:
+            worst = jnp.maximum(worst, e)
+        return worst > 1e-6
+
+    def step(es):
+        xs = [inverse_ref[p] for p in range(patches)]
+        ms = [dot(xs[p], system_ref[p]) for p in range(patches)]
+        ys = [dot(ms[p], xs[p]) for p in range(patches)]
+        for p in range(patches):
+            s = 2.0 * (1.0 + es[p]) / (2.0 + es[p])
+            inverse_ref[p] = (2.0 * s) * xs[p] - (s * s) * ys[p]
+        return tuple(e * e / (4.0 * (1.0 + e)) for e in es)
+
+    lax.while_loop(more, step, tuple(excess))
+    for p in range(patches):
+        z = dot(inverse_ref[p], spreads[p])
+        shift = dot(pulls[p], z)[0:1]
+        out_ref[:, p * PATCH : (p + 1) * PATCH] = (
+            centers[p] + shift + 0.5 * spreads[p] + (0.5 * floor) * z
+        )
+
+
 def analyze(members, cells, observed, variance):
-    ensemble_size = members.shape[0]
-    highest = lax.Precision.HIGHEST
-    center = jnp.mean(members, axis=0)
-    spread = members - center[None, :]
-    obs_spread = jnp.take(spread, cells, axis=1)
-    innovation = observed - jnp.take(center, cells)
-    weighted = obs_spread / variance[None, :]
-    gram = jnp.dot(weighted, obs_spread.T, precision=highest, preferred_element_type=jnp.float32)
-    system = gram + (ensemble_size - 1.0) * jnp.eye(ensemble_size, dtype=jnp.float32)
-    factor = jnp.linalg.cholesky(system)
-    pulled = jnp.dot(weighted, innovation, precision=highest, preferred_element_type=jnp.float32)
-    right_side = jnp.concatenate([pulled[:, None], gram], axis=1)
-    solved = jax.scipy.linalg.cho_solve((factor, True), right_side)
-    gain_mean = solved[:, 0]
-    mixing = solved[:, 1:]
-    transform = jnp.eye(ensemble_size, dtype=jnp.float32) - 0.5 * mixing + gain_mean[None, :]
-    return center[None, :] + jnp.dot(
-        transform, spread, precision=highest, preferred_element_type=jnp.float32
-    )
+    size = members.shape[0]
+    patches = cells.shape[0]
+    return pl.pallas_call(
+        analysis_kernel,
+        out_shape=jax.ShapeDtypeStruct(members.shape, jnp.float32),
+        in_specs=[pl.BlockSpec(memory_space=pltpu.VMEM)] * 4,
+        out_specs=pl.BlockSpec(memory_space=pltpu.VMEM),
+        scratch_shapes=[
+            pltpu.VMEM((patches, size, size), jnp.float32),
+            pltpu.VMEM((patches, size, size), jnp.float32),
+        ],
+    )(members, cells, observed, variance)
 
 
 def on_device(prior_ensemble_fields, vel_y, vel_x, diffus, assign, obs_cell, obs_value, obs_var):
@@ -64,7 +132,6 @@
     columns = tile_rows * width_cells
     groups = lax.axis_size("mem")
     group_columns = columns // groups
-    patches_here = group_columns // PATCH
     ensemble = prior_ensemble_fields
     stacked = jnp.concatenate([ensemble, vel_y[None], vel_x[None], diffus[None]], axis=0)
     widened = extended(stacked, (("tile", 1),), 4)
@@ -82,9 +149,8 @@
     permuted = jnp.take(ensemble.reshape(local_members, columns), order, axis=1)
     blocks = permuted.reshape(local_members, groups, group_columns)
     gathered = lax.all_to_all(blocks, "mem", split_axis=1, concat_axis=0, tiled=True)
-    gathered = gathered.reshape(local_members * groups, patches_here, PATCH)
-    updated = jax.vmap(analyze, in_axes=(1, 0, 0, 0), out_axes=1)(
-        gathered, obs_cell, obs_value, obs_var
+    updated = analyze(
+        gathered.reshape(local_members * groups, group_columns), obs_cell, obs_value, obs_var
     )
     outgoing = updated.reshape(local_members * groups, 1, group_columns)
     returned = lax.all_to_all(outgoing, "mem", split_axis=0, concat_axis=1, tiled=True)

time: 134 us -> 79.8 us (0.60)
  other arithmetic: 58.6 us -> 14.3 us
  local copies, waits for them, and re-layouts: 32.9 us -> 18.1 us
  Pallas kernels: 0 us -> 7.88 us
  matrix products: 3.69 us -> 0 us
  waiting for transfers between devices: 18 us -> 19.5 us
    another operation x6 -> x0, other arithmetic: 43.4 us -> none  [the longest x3 23.6 us: analyze(): factor = jnp.linalg.cholesky(system)]
    gather x3 -> x0, local copies, waits for them, and re-layouts: 15.9 us -> none  [the longest x2 9.12 us: analyze(): innovation = observed - jnp.take(center, cells)]
    pallas_call x0 -> x1, Pallas kernels: none -> 7.88 us  [analyze(): pl.pallas_call(analysis_kernel, out_shape=jax.ShapeDtypeStruct(members.sh...]
    dot_general x3 -> x0, matrix products: 2.91 us -> none  [the longest x1 1.81 us: analyze(): jnp.dot(weighted, obs_spread.T, precision=highest, preferred_element_type...]
  transfers between devices with their start and end apart: 6 -> 6, of which waited for: 6 -> 6; matrix products, arithmetic and copies ran while one was open for 7% -> 10% of each run, Pallas kernels for 0% -> 0%
where the time goes in v1:
time: 79.8 us; the launch traced here: 79.3 us
  waiting for transfers between devices  19.5 us (24%)
  starting transfers between devices  19.4 us (24%)
  local copies, waits for them, and re-layouts  18.1 us (23%)
  other arithmetic  14.3 us (18%)
  Pallas kernels  7.88 us (10%)
    pallas_call x1, Pallas kernels, analyze(): pl.pallas_call(analysis_kernel, out_shape=jax.ShapeDtypeStruct(members.sh...  7.88 us
    ppermute x2, starting transfers between devices, extended(): lax.ppermute(lax.slice_in_dim(block, block.shape[dim] - width, None, axis...  6.35 us
    ppermute x2, starting transfers between devices, extended(): lax.ppermute(lax.slice_in_dim(block, 0, width, axis=dim), axis, backward)  6.23 us
    all_to_all x1, waiting for transfers between devices, on_device(): lax.all_to_all(blocks, 'mem', split_axis=1, concat_axis=0, tiled=True)  5.96 us
    all_to_all x1, waiting for transfers between devices, on_device(): lax.all_to_all(outgoing, 'mem', split_axis=0, concat_axis=1, tiled=True)  5.96 us
    sort x1, other arithmetic, on_device(): positions = jnp.argsort(order)  5.74 us
    gather x1, local copies, waits for them, and re-layouts, on_device(): jnp.take(returned, positions, axis=1)  5.47 us
    gather x1, local copies, waits for them, and re-layouts, on_device(): permuted = jnp.take(ensemble.reshape(local_members, columns), order, axis=1)  5.46 us
  transfers between devices with their start and end apart: 6, of which 6 were waited for; matrix products, arithmetic and copies ran while one was open for 10% of the time, Pallas kernels for 0%

profile of v1, /device:TPU:16, one launch (start us, length us, event | category | flops | bytes accessed | tf_op | source)
XLA Modules:
  0.0 79.3 jit_solution(9839922486845134619)
XLA Ops:
  0.0 1.1 %pad_maximum_fusion.11 = f32[35,4,512]{2,1,0:T(4,128)S(1)} fusion(f32[1,4,512]{2,1,0:T(4,128)} %bitcast.34, f32[1,4,512]{2,1,0:T(4,128)} %bitcast.38, f32[1,4,512]{2,1,0:T(4,128)} %bitcast.42, f32[32,4,512]{2,1,0:T(4,128)} %param.10), kind=kLoop, calls=%fused_computation.33 | loop fusion | flops 215040 | bytes 573440 | tf_op jit(solution)/shard_map/concatenate | solution.py:136
  1.1 3.4 %collective-permute-start = (f32[35,4,512]{2,1,0:T(4,128)S(1)}, f32[35,4,512]{2,1,0:T(4,128)S(1)}, u32[]{:S(2)}, u32[]{:S(2)}) collective-permute-start(f32[35,4,512]{2,1,0:T(4,128)S(1)} %pad_maximum_fusion.11), channel_id=1, source_target_pairs={{0,4},{4,8},{8,12},{12,16},{16,20},{20,24},{24,28},{1,5},{5,9},{9,... | collective-permute-start | bytes 860168 | tf_op jit(solution)/shard_map/ppermute | solution.py:16
  4.5 3.3 %collective-permute-start.1 = (f32[35,4,512]{2,1,0:T(4,128)S(1)}, f32[35,4,512]{2,1,0:T(4,128)S(1)}, u32[]{:S(2)}, u32[]{:S(2)}) collective-permute-start(f32[35,4,512]{2,1,0:T(4,128)S(1)} %pad_maximum_fusion.11), channel_id=1, source_target_pairs={{4,0},{8,4},{12,8},{16,12},{20,16},{24,20},{28,24},{5,1},{9,5},{13... | collective-permute-start | bytes 860168 | tf_op jit(solution)/shard_map/ppermute | solution.py:19
  7.8 0.7 fusion.39
  8.5 0.7 compare_and_fusion.1
  9.2 5.7 %sort.17 = (s32[2048]{0:T(1024)}, s32[2048]{0:T(1024)S(1)}) sort(s32[2048]{0:T(1024)} %bitcast.48, s32[2048]{0:T(1024)S(1)} %iota.10), dimensions={0}, to_apply=%region_0.2 | sort | flops 22528 | bytes 32768 | tf_op jit(solution)/shard_map/jit(argsort)/sort | solution.py:158
  15.0 0.7 broadcast_multiply_fusion
  15.7 1.0 %collective-permute-done = f32[35,4,512]{2,1,0:T(4,128)S(1)} collective-permute-done((f32[35,4,512]{2,1,0:T(4,128)S(1)}, f32[35,4,512]{2,1,0:T(4,128)S(1)}, u32[]{:S(2)}, u32[]{:S(2)}) %collective-permute-start) | collective-permute-done | bytes 286752 | tf_op jit(solution)/shard_map/ppermute | solution.py:16
  16.7 1.9 %collective-permute-done.1 = f32[35,4,512]{2,1,0:T(4,128)S(1)} collective-permute-done((f32[35,4,512]{2,1,0:T(4,128)S(1)}, f32[35,4,512]{2,1,0:T(4,128)S(1)}, u32[]{:S(2)}, u32[]{:S(2)}) %collective-permute-start.1) | collective-permute-done | bytes 286752 | tf_op jit(solution)/shard_map/ppermute | solution.py:19
  18.6 1.2 %pad_maximum_fusion = f32[35,12,512]{2,1,0:T(8,128)S(1)} fusion(f32[35,4,512]{2,1,0:T(4,128)S(1)} %collective-permute-done.1, f32[1,4,512]{2,1,0:T(4,128)} %bitcast.35, f32[1,4,512]{2,1,0:T(4,128)} %bitcast.39, f32[1,4,512]{2,1,0:T(4,128)} %bitcast.43, f32[32,4,512]{2,1,0:T(4,128)} %param.10, f32[35,4,512]{2,1,0:T(4,128)S(1)} %collective-permute-done), kind=kLoop, calls=%fused_computation.2 | loop fusion | flops 1075200 | bytes 1720320 | tf_op jit(solution)/shard_map/concatenate | solution.py:20
  19.8 0.3 fusion.44
  20.1 0.0 copy-start.3
  20.1 0.0 copy-start.4
  20.1 0.3 fusion.41
  20.4 0.1 fusion.42
  20.5 0.1 fusion.43
  20.6 0.4 copy-done
  21.0 0.9 %fusion.5 = f32[32,8,512]{2,1,0:T(8,128)S(1)} fusion(f32[35,4,512]{2,1,0:T(4,128)S(1)} %collective-permute-done, f32[1,4,512]{2,1,0:T(4,128)S(1)} %bitcast.37, f32[1,4,512]{2,1,0:T(4,128)S(1)} %bitcast.41, f32[1,4,512]{2,1,0:T(4,128)S(1)} %bitcast.45, f32[32,4,512]{2,1,0:T(4,128)S(1)} %copy-done, f32[35,4,512]{2,1,0:T(4,128)S(1)} %collective-permute-done.1, ...), kind=kLoop, calls=%fused_computation.9 | loop fusion | flops 4849664 | bytes 5103624 | tf_op jit(solution)/shard_map/jit(_where)/select_n | solution.py:146
  21.9 0.2 fusion.45
  22.1 0.2 fusion.48
  22.4 0.1 fusion.46
  22.5 0.1 fusion.47
  22.6 0.8 %fusion.26 = f32[32,4,512]{2,1,0:T(4,128)S(1)} fusion(f32[32,8,512]{2,1,0:T(8,128)S(1)} %fusion.5, f32[32,4,2]{2,1,0:T(4,128)S(1)} %get-tuple-element.24, f32[32,4,510]{2,1,0:T(4,128)S(1)} %get-tuple-element.26, f32[32,4,510]{2,1,0:T(4,128)S(1)} %get-tuple-element.25, f32[32,4,2]{2,1,0:T(4,128)S(1)} %get-tuple-element.23, ...), kind=kLoop, calls=%fused_computation.50 | loop fusion | flops 1835008 | bytes 2646016 | tf_op jit(solution)/shard_map/add | solution.py:39
  23.4 0.3 copy.26
  23.7 5.5 %gather_fusion = f32[2048,32]{1,0:T(8,128)S(1)} fusion(f32[32,2048]{0,1:T(8,128)S(1)} %bitcast.27, s32[2048]{0:T(1024)S(1)} %fusion.39), kind=kCustom, calls=%fused_computation.clone | custom fusion | bytes 532480 | tf_op jit(solution)/shard_map/jit(_take)/gather | solution.py:149
  29.2 0.3 broadcast_select_fusion.1
  29.6 1.0 %copy.27 = f32[32,4,512]{2,0,1:T(8,128)} copy(f32[32,4,512]{0,2,1:T(8,128)S(1)} %bitcast.29) | data formatting | bytes 524288 | tf_op jit(solution)/shard_map/reshape | solution.py:150
  30.6 3.4 %all-to-all-start = ((f32[32,4,512]{2,0,1:T(8,128)}), f32[32,4,512]{2,0,1:T(8,128)S(1)}, u32[]{:S(2)}, u32[]{:S(2)}) async-start(f32[32,4,512]{2,0,1:T(8,128)} %copy.27), calls=%async_computation | async-start | bytes 524288 | tf_op jit(solution)/shard_map/all_to_all | solution.py:151
  34.0 6.0 %all-to-all-done = f32[32,4,512]{2,0,1:T(8,128)S(1)} async-done(((f32[32,4,512]{2,0,1:T(8,128)}), f32[32,4,512]{2,0,1:T(8,128)S(1)}, u32[]{:S(2)}, u32[]{:S(2)}) %all-to-all-start) | async-done | bytes 262176 | tf_op jit(solution)/shard_map/all_to_all | solution.py:151
  40.0 0.7 copy-done.1
  40.7 7.9 %shard_map.82 = f32[128,512]{1,0:T(8,128)} custom-call(f32[128,512]{1,0:T(8,128)} %bitcast.32, s32[2,512]{1,0:T(2,128)} %cells_ref.1, f32[2,512]{1,0:T(2,128)} %observed_ref.1, f32[2,512]{1,0:T(2,128)} %variance_ref.1), custom_call_target="tpu_custom_call" | custom-call | tf_op jit(solution)/shard_map/pallas_call | solution.py:118
  48.5 1.9 %copy.28 = f32[128,1,512]{2,1,0:T(1,128)} copy(f32[128,1,512]{2,0,1:T(8,128)} %bitcast.33) | data formatting | bytes 524288 | tf_op jit(solution)/shard_map/reshape | solution.py:155
  50.5 3.4 %all-to-all-start.1 = ((f32[128,1,512]{2,1,0:T(1,128)}), f32[128,1,512]{2,1,0:T(1,128)S(1)}, u32[]{:S(2)}, u32[]{:S(2)}) async-start(f32[128,1,512]{2,1,0:T(1,128)} %copy.28), calls=%async_computation.1 | async-start | bytes 524288 | tf_op jit(solution)/shard_map/all_to_all | solution.py:156
  53.9 6.0 %all-to-all-done.1 = f32[128,1,512]{2,1,0:T(1,128)S(1)} async-done(((f32[128,1,512]{2,1,0:T(1,128)}), f32[128,1,512]{2,1,0:T(1,128)S(1)}, u32[]{:S(2)}, u32[]{:S(2)}) %all-to-all-start.1) | async-done | bytes 262176 | tf_op jit(solution)/shard_map/all_to_all | solution.py:156
  59.8 0.3 copy.29
  60.2 5.5 %gather_fusion.1 = f32[2048,32]{1,0:T(8,128)S(1)} fusion(f32[32,2048]{0,1:T(8,128)S(1)} %bitcast.28, s32[2048]{0:T(1024)S(1)} %fusion.40), kind=kCustom, calls=%fused_computation.1.clone | custom fusion | bytes 532480 | tf_op jit(solution)/shard_map/jit(_take)/gather | solution.py:159
  65.7 0.3 broadcast_select_fusion
  66.0 0.3 copy.34
  66.3 0.2 fusion.49
  66.5 0.2 fusion.52
  66.7 0.1 fusion.53
  66.9 0.1 fusion.50
  67.0 2.9 %collective-permute-start.2 = (f32[32,2,512]{2,1,0:T(2,128)S(1)}, f32[32,2,512]{2,1,0:T(2,128)S(1)}, u32[]{:S(2)}, u32[]{:S(2)}) collective-permute-start(f32[32,2,512]{2,1,0:T(2,128)S(1)} %get-tuple-element.36), channel_id=1, source_target_pairs={{4,0},{8,4},{12,8},{16,12},{20,16},{24,20},{28,24},{5,1},{9,5},{13... | collective-permute-start | bytes 393224 | tf_op jit(solution)/shard_map/ppermute | solution.py:19
  69.8 3.0 %collective-permute-start.3 = (f32[32,2,512]{2,1,0:T(2,128)S(1)}, f32[32,2,512]{2,1,0:T(2,128)S(1)}, u32[]{:S(2)}, u32[]{:S(2)}) collective-permute-start(f32[32,2,512]{2,1,0:T(2,128)S(1)} %get-tuple-element.35), channel_id=1, source_target_pairs={{0,4},{4,8},{8,12},{12,16},{16,20},{20,24},{24,28},{1,5},{5,9},{9,... | collective-permute-start | bytes 393224 | tf_op jit(solution)/shard_map/ppermute | solution.py:16
  72.8 0.1 fusion.51
  72.9 0.9 %collective-permute-done.2 = f32[32,2,512]{2,1,0:T(2,128)S(1)} collective-permute-done((f32[32,2,512]{2,1,0:T(2,128)S(1)}, f32[32,2,512]{2,1,0:T(2,128)S(1)}, u32[]{:S(2)}, u32[]{:S(2)}) %collective-permute-start.2) | collective-permute-done | bytes 131104 | tf_op jit(solution)/shard_map/ppermute | solution.py:19
  73.8 3.8 %collective-permute-done.3 = f32[32,2,512]{2,1,0:T(2,128)S(1)} collective-permute-done((f32[32,2,512]{2,1,0:T(2,128)S(1)}, f32[32,2,512]{2,1,0:T(2,128)S(1)}, u32[]{:S(2)}, u32[]{:S(2)}) %collective-permute-start.3) | collective-permute-done | bytes 131104 | tf_op jit(solution)/shard_map/ppermute | solution.py:16
  77.6 1.7 %fusion.22 = f32[32,4,512]{2,1,0:T(4,128)} fusion(f32[32,4,512]{2,1,0:T(4,128)S(1)} %copy.34, f32[32,2,512]{2,1,0:T(2,128)S(1)} %collective-permute-done.2, f32[32,2,512]{2,1,0:T(2,128)S(1)} %collective-permute-done.3, f32[32,4,2]{2,1,0:T(4,128)S(1)} %get-tuple-element.32, f32[32,4,510]{2,1,0:T(4,128)S(1)} %get-tuple-element.34, ...), kind=kLoop, calls=%fused_computation.43 | loop fusion | flops 2097152 | bytes 1859584 | tf_op jit(solution)/shard_map/add | solution.py:39
  (11 shorter events, 0.1 us)
Async XLA Ops:
  1.1 15.6 %collective-permute-start = (f32[35,4,512]{2,1,0:T(4,128)S(1)}, f32[35,4,512]{2,1,0:T(4,128)S(1)}, u32[]{:S(2)}, u32[]{:S(2)}) collective-permute-start(f32[35,4,512]{2,1,0:T(4,128)S(1)} %pad_maximum_fusion.11), channel_id=1, source_target_pairs={{0,4},{4,8},{8,12},{12,16},{16,20},{20,24},{24,28},{1,5},{5,9},{9,... | collective-permute-start | bytes 860168 | tf_op jit(solution)/shard_map/ppermute | solution.py:16
  4.5 14.1 %collective-permute-start.1 = (f32[35,4,512]{2,1,0:T(4,128)S(1)}, f32[35,4,512]{2,1,0:T(4,128)S(1)}, u32[]{:S(2)}, u32[]{:S(2)}) collective-permute-start(f32[35,4,512]{2,1,0:T(4,128)S(1)} %pad_maximum_fusion.11), channel_id=1, source_target_pairs={{4,0},{8,4},{12,8},{16,12},{20,16},{24,20},{28,24},{5,1},{9,5},{13... | collective-permute-start | bytes 860168 | tf_op jit(solution)/shard_map/ppermute | solution.py:19
  20.0 1.0 %copy-start = (f32[32,4,512]{2,1,0:T(4,128)S(1)}, f32[32,4,512]{2,1,0:T(4,128)}, u32[]{:S(2)}) copy-start(f32[32,4,512]{2,1,0:T(4,128)} %param.10) | copy-start | bytes 786436
  20.1 0.9 %copy-start.2 = (f32[4,512]{1,0:T(4,128)S(1)}, f32[4,512]{1,0:T(4,128)}, u32[]{:S(2)}) copy-start(f32[4,512]{1,0:T(4,128)} %param.13) | copy-start | bytes 24580
  20.1 0.9 %copy-start.3 = (f32[4,512]{1,0:T(4,128)S(1)}, f32[4,512]{1,0:T(4,128)}, u32[]{:S(2)}) copy-start(f32[4,512]{1,0:T(4,128)} %param.12) | copy-start | bytes 24580
  20.1 0.9 %copy-start.4 = (f32[4,512]{1,0:T(4,128)S(1)}, f32[4,512]{1,0:T(4,128)}, u32[]{:S(2)}) copy-start(f32[4,512]{1,0:T(4,128)} %param.11) | copy-start | bytes 24580
  30.6 9.4 %all-to-all-start = ((f32[32,4,512]{2,0,1:T(8,128)}), f32[32,4,512]{2,0,1:T(8,128)S(1)}, u32[]{:S(2)}, u32[]{:S(2)}) async-start(f32[32,4,512]{2,0,1:T(8,128)} %copy.27), calls=%async_computation | async-start | bytes 524288 | tf_op jit(solution)/shard_map/all_to_all | solution.py:151
  40.0 0.7 copy-start.1
  50.5 9.4 %all-to-all-start.1 = ((f32[128,1,512]{2,1,0:T(1,128)}), f32[128,1,512]{2,1,0:T(1,128)S(1)}, u32[]{:S(2)}, u32[]{:S(2)}) async-start(f32[128,1,512]{2,1,0:T(1,128)} %copy.28), calls=%async_computation.1 | async-start | bytes 524288 | tf_op jit(solution)/shard_map/all_to_all | solution.py:156
  67.0 6.9 %collective-permute-start.2 = (f32[32,2,512]{2,1,0:T(2,128)S(1)}, f32[32,2,512]{2,1,0:T(2,128)S(1)}, u32[]{:S(2)}, u32[]{:S(2)}) collective-permute-start(f32[32,2,512]{2,1,0:T(2,128)S(1)} %get-tuple-element.36), channel_id=1, source_target_pairs={{4,0},{8,4},{12,8},{16,12},{20,16},{24,20},{28,24},{5,1},{9,5},{13... | collective-permute-start | bytes 393224 | tf_op jit(solution)/shard_map/ppermute | solution.py:19
  69.8 7.8 %collective-permute-start.3 = (f32[32,2,512]{2,1,0:T(2,128)S(1)}, f32[32,2,512]{2,1,0:T(2,128)S(1)}, u32[]{:S(2)}, u32[]{:S(2)}) collective-permute-start(f32[32,2,512]{2,1,0:T(2,128)S(1)} %get-tuple-element.35), channel_id=1, source_target_pairs={{0,4},{4,8},{8,12},{12,16},{16,20},{20,24},{24,28},{1,5},{5,9},{9,... | collective-permute-start | bytes 393224 | tf_op jit(solution)/shard_map/ppermute | solution.py:16

commit v2 on v1

--- a/solution.py
+++ b/solution.py
@@ -1,3 +1,5 @@
+import functools
+
 import jax
 import jax.numpy as jnp
 from jax import lax
@@ -8,35 +10,289 @@
 PATCH = 256
 
 
-def extended(block, sides, width):
-    for axis, dim in sides:
-        count = lax.axis_size(axis)
-        forward = [(i, i + 1) for i in range(count - 1)]
-        backward = [(target, source) for source, target in forward]
-        low = lax.ppermute(
-            lax.slice_in_dim(block, block.shape[dim] - width, None, axis=dim), axis, forward
-        )
-        high = lax.ppermute(lax.slice_in_dim(block, 0, width, axis=dim), axis, backward)
-        block = jnp.concatenate([low, block, high], axis=dim)
-    return block
-
-
-def advance(padded, coef_y, coef_x, coef_k):
-    center = padded[..., 2:-2, :]
-    above = padded[..., 3:-1, :]
-    below = padded[..., 1:-3, :]
-    grad_y = (-padded[..., 4:, :] + 8.0 * above - 8.0 * below + padded[..., :-4, :]) / 12.0
-    lap_y = above - 2.0 * center + below
-    right_one = jnp.roll(center, -1, axis=-1)
-    left_one = jnp.roll(center, 1, axis=-1)
-    grad_x = (
-        -jnp.roll(center, -2, axis=-1)
-        + 8.0 * right_one
-        - 8.0 * left_one
-        + jnp.roll(center, 2, axis=-1)
-    ) / 12.0
-    lap_x = right_one - 2.0 * center + left_one
-    return center - coef_y * grad_y - coef_x * grad_x + coef_k * (lap_y + lap_x)
+MESH = pl.DeviceIdType.MESH
+NN = (((1,), (0,)), ((), ()))
+
+
+def one_step(rows, coef_y, coef_x, coef_k):
+    far_below, below, center, above, far_above = rows
+    width = center.shape[1]
+    grad_y = (far_below - far_above + 8.0 * (above - below)) * (1.0 / 12.0)
+    right_one = pltpu.roll(center, width - 1, 1)
+    left_one = pltpu.roll(center, 1, 1)
+    right_two = pltpu.roll(center, width - 2, 1)
+    left_two = pltpu.roll(center, 2, 1)
+    grad_x = (left_two - right_two + 8.0 * (right_one - left_one)) * (1.0 / 12.0)
+    lap = (above + below) + (right_one + left_one) - 4.0 * center
+    return center - coef_y * grad_y - coef_x * grad_x + coef_k * lap
+
+
+def enter(tile, tiles, me, groups):
+    barrier = pltpu.get_barrier_semaphore()
+    for k in range(1, groups):
+        pl.semaphore_signal(
+            barrier, inc=1, device_id={"mem": lax.rem(me + k, groups)}, device_id_type=MESH
+        )
+
+    @pl.when(tile > 0)
+    def _():
+        pl.semaphore_signal(barrier, inc=1, device_id={"tile": tile - 1}, device_id_type=MESH)
+
+    @pl.when(tile < tiles - 1)
+    def _():
+        pl.semaphore_signal(barrier, inc=1, device_id={"tile": tile + 1}, device_id_type=MESH)
+
+    edges = jnp.where(tile > 0, 1, 0) + jnp.where(tile < tiles - 1, 1, 0)
+    pl.semaphore_wait(barrier, groups - 1 + edges)
+
+
+def build_hot(order_ref, hot_ref):
+    columns = hot_ref.shape[0]
+    block = 128
+
+    def fill(i, carry):
+        start = pl.multiple_of(i * block, block)
+        row = lax.broadcasted_iota(jnp.int32, (block, columns), 0) + start
+        hot_ref[pl.ds(start, block), :] = jnp.where(row == order_ref[...], 1.0, 0.0).astype(
+            jnp.bfloat16
+        )
+        return carry
+
+    lax.fori_loop(0, columns // block, fill, 0)
+
+
+def split_into(parts_ref, value, start):
+    rows, width = value.shape
+    high = value.astype(jnp.bfloat16)
+    rest = value - high.astype(jnp.float32)
+    middle = rest.astype(jnp.bfloat16)
+    low = (rest - middle.astype(jnp.float32)).astype(jnp.bfloat16)
+    for i, part in enumerate((high, middle, low)):
+        parts_ref[i * rows : (i + 1) * rows, start : start + width] = part
+
+
+def picked(parts_ref, hot, dims):
+    wide = lax.dot_general(parts_ref[...], hot, dims, preferred_element_type=jnp.float32)
+    rows = wide.shape[0] // 3
+    return wide[:rows] + (wide[rows : 2 * rows] + wide[2 * rows :])
+
+
+def forecast_kernel(
+    tiles, groups, prior_ref, vy_ref, vx_ref, dk_ref, order_ref, out_ref,
+    below_ref, above_ref, below_c, above_c, hot_ref, parts_ref, outgoing, incoming,
+    up_send, up_recv, down_send, down_recv, mem_send, mem_recv,
+):
+    tile, me = lax.axis_index("tile"), lax.axis_index("mem")
+    members, height, width = prior_ref.shape
+    group_columns = out_ref.shape[1]
+    has_below, has_above = tile > 0, tile < tiles - 1
+    enter(tile, tiles, me, groups)
+
+    def halo(target, field, coefs, send, recv):
+        pairs = [(prior_ref, field)] + [
+            (ref, coefs.at[i]) for i, ref in enumerate((vy_ref, vx_ref, dk_ref))
+        ]
+        return [
+            pltpu.make_async_remote_copy(
+                src_ref=src, dst_ref=dst, send_sem=send.at[i], recv_sem=recv.at[i],
+                device_id={"tile": target}, device_id_type=MESH,
+            )
+            for i, (src, dst) in enumerate(pairs)
+        ]
+
+    up = halo(tile + 1, below_ref, below_c, up_send, up_recv)
+    down = halo(tile - 1, above_ref, above_c, down_send, down_recv)
+
+    @pl.when(has_above)
+    def _():
+        for c in up:
+            c.start()
+
+    @pl.when(has_below)
+    def _():
+        for c in down:
+            c.start()
+
+    @pl.when(jnp.logical_not(has_below))
+    def _():
+        below_ref[...] = jnp.zeros_like(below_ref)
+        below_c[...] = jnp.zeros_like(below_c)
+
+    @pl.when(jnp.logical_not(has_above))
+    def _():
+        above_ref[...] = jnp.zeros_like(above_ref)
+        above_c[...] = jnp.zeros_like(above_c)
+
+    build_hot(order_ref, hot_ref)
+
+    @pl.when(has_below)
+    def _():
+        for c in up:
+            c.wait_recv()
+
+    @pl.when(has_above)
+    def _():
+        for c in down:
+            c.wait_recv()
+
+    def slab(r):
+        if r < 0:
+            return below_ref[:, height + r, :]
+        if r >= height:
+            return above_ref[:, r - height, :]
+        return prior_ref[:, r, :]
+
+    def coefs(r):
+        if r < 0:
+            return [below_c[i, height + r : height + r + 1, :] for i in range(3)]
+        if r >= height:
+            return [above_c[i, r - height : r - height + 1, :] for i in range(3)]
+        return [ref[r : r + 1, :] for ref in (vy_ref, vx_ref, dk_ref)]
+
+    keep_below = jnp.where(has_below, 1.0, 0.0)
+    keep_above = jnp.where(has_above, 1.0, 0.0)
+    middle = {}
+    for r in range(-2, height + 2):
+        value = one_step([slab(r + o) for o in range(-2, 3)], *coefs(r))
+        if r < 0:
+            value = value * keep_below
+        if r >= height:
+            value = value * keep_above
+        middle[r] = value
+    for r in range(height):
+        value = one_step([middle[r + o] for o in range(-2, 3)], *coefs(r))
+        split_into(parts_ref, value, r * width)
+
+    sent = []
+    order = sorted(range(1, groups), key=lambda k: abs(2 * k - groups))
+    for k in order + [0]:
+        target = lax.rem(me + k, groups)
+        first = pl.multiple_of(target * group_columns, group_columns)
+        block = picked(parts_ref, hot_ref[:, pl.ds(first, group_columns)], NN)
+        if k == 0:
+            out_ref[pl.ds(pl.multiple_of(me * members, members), members), :] = block
+            continue
+        outgoing[k - 1] = block
+        c = pltpu.make_async_remote_copy(
+            src_ref=outgoing.at[k - 1], dst_ref=incoming.at[k - 1],
+            send_sem=mem_send.at[k - 1], recv_sem=mem_recv.at[k - 1],
+            device_id={"mem": target}, device_id_type=MESH,
+        )
+        c.start()
+        sent.append((k, c))
+    for k, c in reversed(sent):
+        c.wait_recv()
+        source = lax.rem(me - k + groups, groups)
+        out_ref[pl.ds(pl.multiple_of(source * members, members), members), :] = incoming[k - 1]
+    for k, c in sent:
+        c.wait_send()
+
+    @pl.when(has_above)
+    def _():
+        for c in up:
+            c.wait_send()
+
+    @pl.when(has_below)
+    def _():
+        for c in down:
+            c.wait_send()
+
+
+def return_kernel(
+    tiles, groups, updated_ref, vy_ref, vx_ref, dk_ref, order_ref, out_ref,
+    below_ref, above_ref, rows_ref, hot_ref, incoming, parts_ref, whole_ref,
+    up_send, up_recv, down_send, down_recv, mem_send, mem_recv,
+):
+    tile, me = lax.axis_index("tile"), lax.axis_index("mem")
+    members, height, width = out_ref.shape
+    group_columns = updated_ref.shape[1]
+    has_below, has_above = tile > 0, tile < tiles - 1
+    enter(tile, tiles, me, groups)
+    sent = []
+    for k in sorted(range(1, groups), key=lambda k: abs(2 * k - groups)):
+        target = lax.rem(me + k, groups)
+        c = pltpu.make_async_remote_copy(
+            src_ref=updated_ref.at[pl.ds(pl.multiple_of(target * members, members), members), :],
+            dst_ref=incoming.at[k - 1],
+            send_sem=mem_send.at[k - 1], recv_sem=mem_recv.at[k - 1],
+            device_id={"mem": target}, device_id_type=MESH,
+        )
+        c.start()
+        sent.append((k, c))
+    build_hot(order_ref, hot_ref)
+    own = pl.multiple_of(me * group_columns, group_columns)
+    whole_ref[:, pl.ds(own, group_columns)] = updated_ref[
+        pl.ds(pl.multiple_of(me * members, members), members), :
+    ]
+    for k, c in reversed(sent):
+        c.wait_recv()
+        source = lax.rem(me - k + groups, groups)
+        first = pl.multiple_of(source * group_columns, group_columns)
+        whole_ref[:, pl.ds(first, group_columns)] = incoming[k - 1]
+    for g in range(groups):
+        start = g * group_columns
+        split_into(parts_ref, whole_ref[:, start : start + group_columns], start)
+
+    up = pltpu.make_async_remote_copy(
+        src_ref=rows_ref.at[pl.ds(height - 2, 2)], dst_ref=below_ref,
+        send_sem=up_send, recv_sem=up_recv, device_id={"tile": tile + 1}, device_id_type=MESH,
+    )
+    down = pltpu.make_async_remote_copy(
+        src_ref=rows_ref.at[pl.ds(0, 2)], dst_ref=above_ref,
+        send_sem=down_send, recv_sem=down_recv, device_id={"tile": tile - 1}, device_id_type=MESH,
+    )
+    for r in range(height):
+        rows_ref[r] = picked(parts_ref, hot_ref[r * width : (r + 1) * width, :], NT)
+        if r == 1:
+
+            @pl.when(has_below)
+            def _():
+                down.start()
+
+        if r == height - 1:
+
+            @pl.when(has_above)
+            def _():
+                up.start()
+
+    @pl.when(jnp.logical_not(has_below))
+    def _():
+        below_ref[...] = jnp.zeros_like(below_ref)
+
+    @pl.when(jnp.logical_not(has_above))
+    def _():
+        above_ref[...] = jnp.zeros_like(above_ref)
+
+    @pl.when(has_above)
+    def _():
+        down.wait_recv()
+
+    @pl.when(has_below)
+    def _():
+        up.wait_recv()
+
+    def slab(r):
+        if r < 0:
+            return below_ref[2 + r]
+        if r >= height:
+            return above_ref[r - height]
+        return rows_ref[r]
+
+    for r in range(height):
+        out_ref[:, r, :] = one_step(
+            [slab(r + o) for o in range(-2, 3)],
+            *[ref[r : r + 1, :] for ref in (vy_ref, vx_ref, dk_ref)],
+        )
+    for k, c in sent:
+        c.wait_send()
+
+    @pl.when(has_below)
+    def _():
+        down.wait_send()
+
+    @pl.when(has_above)
+    def _():
+        up.wait_send()
 
 
 def dot(a, b, dims=(((1,), (0,)), ((), ()))):
@@ -128,37 +384,49 @@
 
 
 def on_device(prior_ensemble_fields, vel_y, vel_x, diffus, assign, obs_cell, obs_value, obs_var):
-    local_members, tile_rows, width_cells = prior_ensemble_fields.shape
-    columns = tile_rows * width_cells
-    groups = lax.axis_size("mem")
+    members, height, width = prior_ensemble_fields.shape
+    columns = height * width
+    tiles, groups = lax.axis_size("tile"), lax.axis_size("mem")
     group_columns = columns // groups
-    ensemble = prior_ensemble_fields
-    stacked = jnp.concatenate([ensemble, vel_y[None], vel_x[None], diffus[None]], axis=0)
-    widened = extended(stacked, (("tile", 1),), 4)
-    field_rows = widened[:local_members]
-    near_y = widened[local_members, 2:-2]
-    near_x = widened[local_members + 1, 2:-2]
-    near_k = widened[local_members + 2, 2:-2]
-    middle = advance(field_rows, near_y, near_x, near_k)
-    first_row = lax.axis_index("tile") * tile_rows - 2
-    global_rows = first_row + jnp.arange(tile_rows + 4, dtype=jnp.int32)
-    inside = (global_rows >= 0) & (global_rows < tile_rows * lax.axis_size("tile"))
-    middle = jnp.where(inside[None, :, None], middle, 0.0)
-    ensemble = advance(middle, vel_y, vel_x, diffus)
-    order = assign[0]
-    permuted = jnp.take(ensemble.reshape(local_members, columns), order, axis=1)
-    blocks = permuted.reshape(local_members, groups, group_columns)
-    gathered = lax.all_to_all(blocks, "mem", split_axis=1, concat_axis=0, tiled=True)
-    updated = analyze(
-        gathered.reshape(local_members * groups, group_columns), obs_cell, obs_value, obs_var
-    )
-    outgoing = updated.reshape(local_members * groups, 1, group_columns)
-    returned = lax.all_to_all(outgoing, "mem", split_axis=0, concat_axis=1, tiled=True)
-    returned = returned.reshape(local_members, columns)
-    positions = jnp.argsort(order)
-    analysed = jnp.take(returned, positions, axis=1).reshape(local_members, tile_rows, width_cells)
-    padded = extended(analysed, (("tile", 1),), 2)
-    return advance(padded, vel_y, vel_x, diffus)
+    vmem = pl.BlockSpec(memory_space=pltpu.VMEM)
+    f32, bf16 = jnp.float32, jnp.bfloat16
+    dma = pltpu.SemaphoreType.DMA
+    gathered = pl.pallas_call(
+        functools.partial(forecast_kernel, tiles, groups),
+        out_shape=jax.ShapeDtypeStruct((members * groups, group_columns), f32),
+        in_specs=[vmem] * 5,
+        out_specs=vmem,
+        scratch_shapes=[
+            pltpu.VMEM((members, height, width), f32),
+            pltpu.VMEM((members, height, width), f32),
+            pltpu.VMEM((3, height, width), f32),
+            pltpu.VMEM((3, height, width), f32),
+            pltpu.VMEM((columns, columns), bf16),
+            pltpu.VMEM((3 * members, columns), bf16),
+            pltpu.VMEM((groups - 1, members, group_columns), f32),
+            pltpu.VMEM((groups - 1, members, group_columns), f32),
+            dma((4,)), dma((4,)), dma((4,)), dma((4,)), dma((groups - 1,)), dma((groups - 1,)),
+        ],
+        compiler_params=pltpu.CompilerParams(collective_id=0, has_side_effects=True),
+    )(prior_ensemble_fields, vel_y, vel_x, diffus, assign)
+    updated = analyze(gathered, obs_cell, obs_value, obs_var)
+    return pl.pallas_call(
+        functools.partial(return_kernel, tiles, groups),
+        out_shape=jax.ShapeDtypeStruct((members, height, width), f32),
+        in_specs=[vmem] * 5,
+        out_specs=vmem,
+        scratch_shapes=[
+            pltpu.VMEM((2, members, width), f32),
+            pltpu.VMEM((2, members, width), f32),
+            pltpu.VMEM((height, members, width), f32),
+            pltpu.VMEM((columns, columns), bf16),
+            pltpu.VMEM((groups - 1, members, group_columns), f32),
+            pltpu.VMEM((3 * members, columns), bf16),
+            pltpu.VMEM((members, columns), f32),
+            dma, dma, dma, dma, dma((groups - 1,)), dma((groups - 1,)),
+        ],
+        compiler_params=pltpu.CompilerParams(collective_id=1, has_side_effects=True),
+    )(updated, vel_y, vel_x, diffus, assign)
 
 
 def solution(mesh):

time: 79.8 us -> 51.9 us (0.65)
  Pallas kernels: 7.88 us -> 50 us
  waiting for transfers between devices: 19.5 us -> 0 us
  starting transfers between devices: 19.4 us -> 0 us
  local copies, waits for them, and re-layouts: 18.1 us -> 1.67 us
  other arithmetic: 14.3 us -> 0 us
    pallas_call x0 -> x2, Pallas kernels: none -> 42.1 us  [the longest x1 23.8 us: on_device(): pl.pallas_call(functools.partial(forecast_kernel, tiles, groups), out_sha...]
    ppermute x4 -> x0, starting transfers between devices: 12.6 us -> none  [the longest x2 6.35 us: extended(): lax.ppermute(lax.slice_in_dim(block, block.shape[dim] - width, None, axis...]
    all_to_all x2 -> x0, waiting for transfers between devices: 11.9 us -> none  [the longest x1 5.96 us: on_device(): lax.all_to_all(blocks, 'mem', split_axis=1, concat_axis=0, tiled=True)]
    gather x2 -> x0, local copies, waits for them, and re-layouts: 10.9 us -> none  [the longest x1 5.47 us: on_device(): jnp.take(returned, positions, axis=1)]
    ppermute x4 -> x0, waiting for transfers between devices: 7.57 us -> none  [the longest x2 4.78 us: extended(): lax.ppermute(lax.slice_in_dim(block, block.shape[dim] - width, None, axis...]
    all_to_all x2 -> x0, starting transfers between devices: 6.81 us -> none  [the longest x1 3.41 us: on_device(): lax.all_to_all(blocks, 'mem', split_axis=1, concat_axis=0, tiled=True)]
    sort x1 -> x0, other arithmetic: 5.74 us -> none  [on_device(): positions = jnp.argsort(order)]
    reshape x3 -> x0, local copies, waits for them, and re-layouts: 3.26 us -> none  [the longest x1 1.92 us: on_device(): outgoing = updated.reshape(local_members * groups, 1, group_columns)]
  transfers between devices with their start and end apart: 6 -> 0, of which waited for: 6 -> 0; matrix products, arithmetic and copies ran while one was open for 10% -> 0% of each run, Pallas kernels for 0% -> 0%
where the time goes in v2:
time: 51.9 us; the launch traced here: 51.7 us
  Pallas kernels  50 us (96%)
  local copies, waits for them, and re-layouts  1.67 us (3%)
    pallas_call x1, Pallas kernels, on_device(): pl.pallas_call(functools.partial(forecast_kernel, tiles, groups), out_sha...  23.8 us
    pallas_call x1, Pallas kernels, on_device(): pl.pallas_call(functools.partial(return_kernel, tiles, groups), out_shape...  18.3 us
    pallas_call x1, Pallas kernels, analyze(): pl.pallas_call(analysis_kernel, out_shape=jax.ShapeDtypeStruct(members.sh...  7.88 us
    unnamed x1, local copies, waits for them, and re-layouts  1.67 us

profile of v2, /device:TPU:16, one launch (start us, length us, event | category | flops | bytes accessed | tf_op | source)
XLA Modules:
  0.0 51.7 jit_solution(9250281630859248615)
XLA Ops:
  0.0 23.8 %shard_map.82.members_ref = f32[128,512]{1,0:T(8,128)} custom-call(f32[32,4,512]{2,1,0:T(4,128)} %prior_ref.1, f32[4,512]{1,0:T(4,128)} %vy_ref.3, f32[4,512]{1,0:T(4,128)} %vx_ref.3, f32[4,512]{1,0:T(4,128)} %dk_ref.3, s32[1,2048]{1,0:T(1,128)} %order_ref.3), custom_call_target="tpu_custom_call" | custom-call | tf_op jit(solution)/shard_map/pallas_call | solution.py:394
  23.8 7.9 %shard_map.83.updated_ref = f32[128,512]{1,0:T(8,128)} custom-call(f32[128,512]{1,0:T(8,128)} %shard_map.82.members_ref, s32[2,512]{1,0:T(2,128)} %cells_ref.1, f32[2,512]{1,0:T(2,128)} %observed_ref.1, f32[2,512]{1,0:T(2,128)} %variance_ref.1), custom_call_target="tpu_custom_call" | custom-call | tf_op jit(solution)/shard_map/pallas_call | solution.py:374
  31.7 18.3 %shard_map.84 = f32[32,4,512]{2,1,0:T(4,128)} custom-call(f32[128,512]{1,0:T(8,128)} %shard_map.83.updated_ref, f32[4,512]{1,0:T(4,128)} %vy_ref.3, f32[4,512]{1,0:T(4,128)} %vx_ref.3, f32[4,512]{1,0:T(4,128)} %dk_ref.3, s32[1,2048]{1,0:T(1,128)} %order_ref.3), custom_call_target="tpu_custom_call" | custom-call | tf_op jit(solution)/shard_map/pallas_call | solution.py:413
  50.0 1.7 %copy.10 = f32[32,4,512]{2,1,0:T(4,128)} copy(f32[32,4,512]{2,1,0:T(4,128)} %shard_map.84) | data formatting | bytes 524288

commit v3 on v2

--- a/solution.py
+++ b/solution.py
@@ -61,24 +61,50 @@
     lax.fori_loop(0, columns // block, fill, 0)
 
 
-def split_into(parts_ref, value, start):
-    rows, width = value.shape
+def parts_of(value):
     high = value.astype(jnp.bfloat16)
-    rest = value - high.astype(jnp.float32)
-    middle = rest.astype(jnp.bfloat16)
-    low = (rest - middle.astype(jnp.float32)).astype(jnp.bfloat16)
-    for i, part in enumerate((high, middle, low)):
-        parts_ref[i * rows : (i + 1) * rows, start : start + width] = part
-
-
-def picked(parts_ref, hot, dims):
-    wide = lax.dot_general(parts_ref[...], hot, dims, preferred_element_type=jnp.float32)
-    rows = wide.shape[0] // 3
-    return wide[:rows] + (wide[rows : 2 * rows] + wide[2 * rows :])
+    low = (value - high.astype(jnp.float32)).astype(jnp.bfloat16)
+    return jnp.concatenate([high, low], axis=0)
+
+
+def picked(parts, hot):
+    wide = lax.dot_general(parts, hot, NN, preferred_element_type=jnp.float32)
+    rows = wide.shape[0] // 2
+    return wide[:rows] + wide[rows:]
+
+
+def build_inverse_hot(order_ref, hot_ref):
+    columns = hot_ref.shape[0]
+    block = 128
+    across = jnp.concatenate(
+        [order_ref[:, i * block : (i + 1) * block] for i in range(columns // block)], axis=0
+    )
+    across = jnp.concatenate([across] * (block // across.shape[0]), axis=0)
+    down = across.T
+    place = lax.broadcasted_iota(jnp.int32, (block, columns), 1)
+    for i in range(columns // block):
+        hot_ref[i * block : (i + 1) * block, :] = jnp.where(
+            place == down[:, i : i + 1], 1.0, 0.0
+        ).astype(jnp.bfloat16)
+
+
+def observation_sums(cells_ref, observed_ref, variance_ref, sums_ref):
+    patches, nobs = cells_ref.shape
+    for p in range(patches):
+        hot = jnp.where(
+            lax.broadcasted_iota(jnp.int32, (PATCH, nobs), 0) == cells_ref[p : p + 1, :], 1.0, 0.0
+        )
+        inverse_var = 1.0 / variance_ref[p : p + 1, :]
+        pair = jnp.concatenate(
+            [inverse_var, observed_ref[p : p + 1, :] * inverse_var, jnp.zeros((6, nobs), jnp.float32)],
+            axis=0,
+        )
+        sums_ref[8 * p : 8 * (p + 1), :] = dot(pair, hot, NT)
 
 
 def forecast_kernel(
-    tiles, groups, prior_ref, vy_ref, vx_ref, dk_ref, order_ref, out_ref,
+    tiles, groups, prior_ref, vy_ref, vx_ref, dk_ref, order_ref,
+    cells_ref, observed_ref, variance_ref, out_ref, sums_ref,
     below_ref, above_ref, below_c, above_c, hot_ref, parts_ref, outgoing, incoming,
     up_send, up_recv, down_send, down_recv, mem_send, mem_recv,
 ):
@@ -124,6 +150,7 @@
         above_c[...] = jnp.zeros_like(above_c)
 
     build_hot(order_ref, hot_ref)
+    observation_sums(cells_ref, observed_ref, variance_ref, sums_ref)
 
     @pl.when(has_below)
     def _():
@@ -161,14 +188,14 @@
         middle[r] = value
     for r in range(height):
         value = one_step([middle[r + o] for o in range(-2, 3)], *coefs(r))
-        split_into(parts_ref, value, r * width)
+        parts_ref[:, r * width : (r + 1) * width] = parts_of(value)
 
     sent = []
     order = sorted(range(1, groups), key=lambda k: abs(2 * k - groups))
     for k in order + [0]:
         target = lax.rem(me + k, groups)
         first = pl.multiple_of(target * group_columns, group_columns)
-        block = picked(parts_ref, hot_ref[:, pl.ds(first, group_columns)], NN)
+        block = picked(parts_ref[...], hot_ref[:, pl.ds(first, group_columns)])
         if k == 0:
             out_ref[pl.ds(pl.multiple_of(me * members, members), members), :] = block
             continue
@@ -199,12 +226,13 @@
 
 
 def return_kernel(
-    tiles, groups, updated_ref, vy_ref, vx_ref, dk_ref, order_ref, out_ref,
-    below_ref, above_ref, rows_ref, hot_ref, incoming, parts_ref, whole_ref,
+    tiles, groups, updated_ref, order_ref, out_ref,
+    below_ref, above_ref, rows_ref, hot_ref, incoming,
     up_send, up_recv, down_send, down_recv, mem_send, mem_recv,
 ):
     tile, me = lax.axis_index("tile"), lax.axis_index("mem")
-    members, height, width = out_ref.shape
+    extent, members, width = out_ref.shape
+    height = extent - 4
     group_columns = updated_ref.shape[1]
     has_below, has_above = tile > 0, tile < tiles - 1
     enter(tile, tiles, me, groups)
@@ -219,20 +247,7 @@
         )
         c.start()
         sent.append((k, c))
-    build_hot(order_ref, hot_ref)
-    own = pl.multiple_of(me * group_columns, group_columns)
-    whole_ref[:, pl.ds(own, group_columns)] = updated_ref[
-        pl.ds(pl.multiple_of(me * members, members), members), :
-    ]
-    for k, c in reversed(sent):
-        c.wait_recv()
-        source = lax.rem(me - k + groups, groups)
-        first = pl.multiple_of(source * group_columns, group_columns)
-        whole_ref[:, pl.ds(first, group_columns)] = incoming[k - 1]
-    for g in range(groups):
-        start = g * group_columns
-        split_into(parts_ref, whole_ref[:, start : start + group_columns], start)
-
+    build_inverse_hot(order_ref, hot_ref)
     up = pltpu.make_async_remote_copy(
         src_ref=rows_ref.at[pl.ds(height - 2, 2)], dst_ref=below_ref,
         send_sem=up_send, recv_sem=up_recv, device_id={"tile": tile + 1}, device_id_type=MESH,
@@ -241,48 +256,62 @@
         src_ref=rows_ref.at[pl.ds(0, 2)], dst_ref=above_ref,
         send_sem=down_send, recv_sem=down_recv, device_id={"tile": tile - 1}, device_id_type=MESH,
     )
+
+    def share(source, value, r):
+        first = pl.multiple_of(source * group_columns, group_columns)
+        return picked(value, hot_ref[pl.ds(first, group_columns), r * width : (r + 1) * width])
+
+    own = parts_of(updated_ref[pl.ds(pl.multiple_of(me * members, members), members), :])
+    totals = [share(me, own, r) for r in range(height)]
+    for k, c in list(reversed(sent)):
+        c.wait_recv()
+        source = lax.rem(me - k + groups, groups)
+        value = parts_of(incoming[k - 1])
+        last = k == sent[0][0]
+        for r in range(height):
+            totals[r] = totals[r] + share(source, value, r)
+            if not last:
+                continue
+            rows_ref[r] = totals[r]
+            if r == 1:
+
+                @pl.when(has_below)
+                def _():
+                    down.start()
+
+            if r == height - 1:
+
+                @pl.when(has_above)
+                def _():
+                    up.start()
+
     for r in range(height):
-        rows_ref[r] = picked(parts_ref, hot_ref[r * width : (r + 1) * width, :], NT)
-        if r == 1:
-
-            @pl.when(has_below)
-            def _():
-                down.start()
-
-        if r == height - 1:
-
-            @pl.when(has_above)
-            def _():
-                up.start()
+        out_ref[r + 2] = totals[r]
+
+    @pl.when(has_above)
+    def _():
+        down.wait_recv()
+
+    @pl.when(has_below)
+    def _():
+        up.wait_recv()
+
+    @pl.when(has_below)
+    def _():
+        out_ref[0:2] = below_ref[...]
 
     @pl.when(jnp.logical_not(has_below))
     def _():
-        below_ref[...] = jnp.zeros_like(below_ref)
+        out_ref[0:2] = jnp.zeros_like(below_ref)
+
+    @pl.when(has_above)
+    def _():
+        out_ref[height + 2 : height + 4] = above_ref[...]
 
     @pl.when(jnp.logical_not(has_above))
     def _():
-        above_ref[...] = jnp.zeros_like(above_ref)
-
-    @pl.when(has_above)
-    def _():
-        down.wait_recv()
-
-    @pl.when(has_below)
-    def _():
-        up.wait_recv()
-
-    def slab(r):
-        if r < 0:
-            return below_ref[2 + r]
-        if r >= height:
-            return above_ref[r - height]
-        return rows_ref[r]
-
-    for r in range(height):
-        out_ref[:, r, :] = one_step(
-            [slab(r + o) for o in range(-2, 3)],
-            *[ref[r : r + 1, :] for ref in (vy_ref, vx_ref, dk_ref)],
-        )
+        out_ref[height + 2 : height + 4] = jnp.zeros_like(above_ref)
+
     for k, c in sent:
         c.wait_send()
 
@@ -293,6 +322,14 @@
     @pl.when(has_above)
     def _():
         up.wait_send()
+
+
+def last_kernel(rows_ref, vy_ref, vx_ref, dk_ref, out_ref):
+    for r in range(out_ref.shape[1]):
+        out_ref[:, r, :] = one_step(
+            [rows_ref[r + o] for o in range(5)],
+            *[ref[r : r + 1, :] for ref in (vy_ref, vx_ref, dk_ref)],
+        )
 
 
 def dot(a, b, dims=(((1,), (0,)), ((), ()))):
@@ -304,9 +341,9 @@
 NT = (((1,), (1,)), ((), ()))
 
 
-def analysis_kernel(members_ref, cells_ref, observed_ref, variance_ref, out_ref, system_ref, inverse_ref):
+def analysis_kernel(members_ref, sums_ref, out_ref, system_ref, inverse_ref):
     size = members_ref.shape[0]
-    patches = cells_ref.shape[0]
+    patches = members_ref.shape[1] // PATCH
     floor = size - 1.0
     eye = jnp.where(
         lax.broadcasted_iota(jnp.int32, (size, size), 0)
@@ -319,18 +356,7 @@
         x = members_ref[:, p * PATCH : (p + 1) * PATCH]
         center = jnp.mean(x, axis=0, keepdims=True)
         spread = x - center
-        cells = cells_ref[p : p + 1, :]
-        nobs = cells.shape[1]
-        hot = jnp.where(
-            lax.broadcasted_iota(jnp.int32, (PATCH, nobs), 0) == cells, 1.0, 0.0
-        )
-        inverse_var = 1.0 / variance_ref[p : p + 1, :]
-        pair = jnp.concatenate(
-            [inverse_var, observed_ref[p : p + 1, :] * inverse_var, jnp.zeros((6, nobs), jnp.float32)],
-            axis=0,
-        )
-        sums = dot(pair, hot, NT)
-        d, w = sums[0:1], sums[1:2]
+        d, w = sums_ref[8 * p : 8 * p + 1, :], sums_ref[8 * p + 1 : 8 * p + 2, :]
         gram = dot(spread * d, spread, NT)
         pulled = dot(jnp.broadcast_to(w - d * center, (8, PATCH)), spread, NT)
         bound = jnp.max(jnp.sum(jnp.abs(gram), axis=0, keepdims=True)) * 1.0001
@@ -368,19 +394,19 @@
         )
 
 
-def analyze(members, cells, observed, variance):
+def analyze(members, sums):
     size = members.shape[0]
-    patches = cells.shape[0]
+    patches = members.shape[1] // PATCH
     return pl.pallas_call(
         analysis_kernel,
         out_shape=jax.ShapeDtypeStruct(members.shape, jnp.float32),
-        in_specs=[pl.BlockSpec(memory_space=pltpu.VMEM)] * 4,
+        in_specs=[pl.BlockSpec(memory_space=pltpu.VMEM)] * 2,
         out_specs=pl.BlockSpec(memory_space=pltpu.VMEM),
         scratch_shapes=[
             pltpu.VMEM((patches, size, size), jnp.float32),
             pltpu.VMEM((patches, size, size), jnp.float32),
         ],
-    )(members, cells, observed, variance)
+    )(members, sums)
 
 
 def on_device(prior_ensemble_fields, vel_y, vel_x, diffus, assign, obs_cell, obs_value, obs_var):
@@ -391,29 +417,33 @@
     vmem = pl.BlockSpec(memory_space=pltpu.VMEM)
     f32, bf16 = jnp.float32, jnp.bfloat16
     dma = pltpu.SemaphoreType.DMA
-    gathered = pl.pallas_call(
+    patches = obs_cell.shape[0]
+    gathered, sums = pl.pallas_call(
         functools.partial(forecast_kernel, tiles, groups),
-        out_shape=jax.ShapeDtypeStruct((members * groups, group_columns), f32),
-        in_specs=[vmem] * 5,
-        out_specs=vmem,
+        out_shape=(
+            jax.ShapeDtypeStruct((members * groups, group_columns), f32),
+            jax.ShapeDtypeStruct((8 * patches, PATCH), f32),
+        ),
+        in_specs=[vmem] * 8,
+        out_specs=(vmem, vmem),
         scratch_shapes=[
             pltpu.VMEM((members, height, width), f32),
             pltpu.VMEM((members, height, width), f32),
             pltpu.VMEM((3, height, width), f32),
             pltpu.VMEM((3, height, width), f32),
             pltpu.VMEM((columns, columns), bf16),
-            pltpu.VMEM((3 * members, columns), bf16),
+            pltpu.VMEM((2 * members, columns), bf16),
             pltpu.VMEM((groups - 1, members, group_columns), f32),
             pltpu.VMEM((groups - 1, members, group_columns), f32),
             dma((4,)), dma((4,)), dma((4,)), dma((4,)), dma((groups - 1,)), dma((groups - 1,)),
         ],
         compiler_params=pltpu.CompilerParams(collective_id=0, has_side_effects=True),
-    )(prior_ensemble_fields, vel_y, vel_x, diffus, assign)
-    updated = analyze(gathered, obs_cell, obs_value, obs_var)
-    return pl.pallas_call(
+    )(prior_ensemble_fields, vel_y, vel_x, diffus, assign, obs_cell, obs_value, obs_var)
+    updated = analyze(gathered, sums)
+    rows = pl.pallas_call(
         functools.partial(return_kernel, tiles, groups),
-        out_shape=jax.ShapeDtypeStruct((members, height, width), f32),
-        in_specs=[vmem] * 5,
+        out_shape=jax.ShapeDtypeStruct((height + 4, members, width), f32),
+        in_specs=[vmem] * 2,
         out_specs=vmem,
         scratch_shapes=[
             pltpu.VMEM((2, members, width), f32),
@@ -421,12 +451,16 @@
             pltpu.VMEM((height, members, width), f32),
             pltpu.VMEM((columns, columns), bf16),
             pltpu.VMEM((groups - 1, members, group_columns), f32),
-            pltpu.VMEM((3 * members, columns), bf16),
-            pltpu.VMEM((members, columns), f32),
             dma, dma, dma, dma, dma((groups - 1,)), dma((groups - 1,)),
         ],
         compiler_params=pltpu.CompilerParams(collective_id=1, has_side_effects=True),
-    )(updated, vel_y, vel_x, diffus, assign)
+    )(updated, assign)
+    return pl.pallas_call(
+        last_kernel,
+        out_shape=jax.ShapeDtypeStruct((members, height, width), f32),
+        in_specs=[vmem] * 4,
+        out_specs=vmem,
+    )(rows, vel_y, vel_x, diffus)
 
 
 def solution(mesh):

time: 51.9 us -> 49.3 us (0.950)
  local copies, waits for them, and re-layouts: 1.67 us -> 0 us
  Pallas kernels: 50 us -> 48.8 us
    pallas_call x0 -> x1, Pallas kernels: none -> 2.16 us  [on_device(): pl.pallas_call(last_kernel, out_shape=jax.ShapeDtypeStruct((members, heig...]
    pallas_call x1, Pallas kernels: 18.3 us -> 16.5 us  [on_device(): pl.pallas_call(functools.partial(return_kernel, tiles, groups), out_shape...]
    unnamed x1 -> x0, local copies, waits for them, and re-layouts: 1.67 us -> none
    pallas_call x1, Pallas kernels: 7.88 us -> 6.38 us  [analyze(): pl.pallas_call(analysis_kernel, out_shape=jax.ShapeDtypeStruct(members.sh...]
where the time goes in v3:
time: 49.3 us; the launch traced here: 48.8 us
  Pallas kernels  48.8 us (99%)
    pallas_call x1, Pallas kernels, on_device(): pl.pallas_call(functools.partial(forecast_kernel, tiles, groups), out_sha...  23.8 us
    pallas_call x1, Pallas kernels, on_device(): pl.pallas_call(functools.partial(return_kernel, tiles, groups), out_shape...  16.5 us
    pallas_call x1, Pallas kernels, analyze(): pl.pallas_call(analysis_kernel, out_shape=jax.ShapeDtypeStruct(members.sh...  6.38 us
    pallas_call x1, Pallas kernels, on_device(): pl.pallas_call(last_kernel, out_shape=jax.ShapeDtypeStruct((members, heig...  2.16 us

profile of v3, /device:TPU:16, one launch (start us, length us, event | category | flops | bytes accessed | tf_op | source)
XLA Modules:
  0.0 48.8 jit_solution(9072393858780760757)
XLA Ops:
  0.0 23.8 %shard_map.82 = (f32[128,512]{1,0:T(8,128)}, f32[16,256]{1,0:T(8,128)}) custom-call(f32[32,4,512]{2,1,0:T(4,128)} %prior_ref.1, f32[4,512]{1,0:T(4,128)} %vy_ref.3, f32[4,512]{1,0:T(4,128)} %vx_ref.3, f32[4,512]{1,0:T(4,128)} %dk_ref.3, s32[1,2048]{1,0:T(1,128)} %order_ref.3, s32[2,512]{1,0:T(2,128)} %cells_ref.1, f32[2,512]{1,0:T(2,128)} %observed_ref.1, ...), custom_call_target="tpu_custom_call" | custom-call | tf_op jit(solution)/shard_map/pallas_call | solution.py:421
  23.8 6.4 %shard_map.83.updated_ref = f32[128,512]{1,0:T(8,128)} custom-call(f32[128,512]{1,0:T(8,128)} %get-tuple-element.7.members_ref, f32[16,256]{1,0:T(8,128)} %get-tuple-element.8.sums_ref), custom_call_target="tpu_custom_call" | custom-call | tf_op jit(solution)/shard_map/pallas_call | solution.py:400
  30.2 16.5 %shard_map.84.rows_ref = f32[8,32,512]{2,1,0:T(8,128)} custom-call(f32[128,512]{1,0:T(8,128)} %shard_map.83.updated_ref, s32[1,2048]{1,0:T(1,128)} %order_ref.3), custom_call_target="tpu_custom_call" | custom-call | tf_op jit(solution)/shard_map/pallas_call | solution.py:443
  46.7 2.2 %shard_map.85 = f32[32,4,512]{2,1,0:T(4,128)} custom-call(f32[8,32,512]{2,1,0:T(8,128)} %shard_map.84.rows_ref, f32[4,512]{1,0:T(4,128)} %vy_ref.3, f32[4,512]{1,0:T(4,128)} %vx_ref.3, f32[4,512]{1,0:T(4,128)} %dk_ref.3), custom_call_target="tpu_custom_call" | custom-call | tf_op jit(solution)/shard_map/pallas_call | solution.py:458

commit v4 on v3

--- a/solution.py
+++ b/solution.py
@@ -10,6 +10,7 @@
 PATCH = 256
 
 
+CHUNKS = 4
 MESH = pl.DeviceIdType.MESH
 NN = (((1,), (0,)), ((), ()))
 
@@ -27,26 +28,26 @@
     return center - coef_y * grad_y - coef_x * grad_x + coef_k * lap
 
 
-def enter(tile, tiles, me, groups):
+def enter(tile, tiles, me, groups, peers):
     barrier = pltpu.get_barrier_semaphore()
     for k in range(1, groups):
         pl.semaphore_signal(
             barrier, inc=1, device_id={"mem": lax.rem(me + k, groups)}, device_id_type=MESH
         )
-
-    @pl.when(tile > 0)
-    def _():
-        pl.semaphore_signal(barrier, inc=1, device_id={"tile": tile - 1}, device_id_type=MESH)
-
-    @pl.when(tile < tiles - 1)
-    def _():
-        pl.semaphore_signal(barrier, inc=1, device_id={"tile": tile + 1}, device_id_type=MESH)
-
-    edges = jnp.where(tile > 0, 1, 0) + jnp.where(tile < tiles - 1, 1, 0)
-    pl.semaphore_wait(barrier, groups - 1 + edges)
-
-
-def build_hot(order_ref, hot_ref):
+    count = groups - 1
+    for offset in peers:
+        peer = tile + offset
+        there = jnp.logical_and(peer >= 0, peer < tiles)
+        count = count + jnp.where(there, 1, 0)
+
+        @pl.when(there)
+        def _():
+            pl.semaphore_signal(barrier, inc=1, device_id={"tile": peer}, device_id_type=MESH)
+
+    pl.semaphore_wait(barrier, count)
+
+
+def build_hot(order_ref, hot_ref, part, count):
     columns = hot_ref.shape[0]
     block = 128
 
@@ -58,7 +59,8 @@
         )
         return carry
 
-    lax.fori_loop(0, columns // block, fill, 0)
+    steps = columns // block // count
+    lax.fori_loop(part * steps, (part + 1) * steps, fill, 0)
 
 
 def parts_of(value):
@@ -105,19 +107,24 @@
 def forecast_kernel(
     tiles, groups, prior_ref, vy_ref, vx_ref, dk_ref, order_ref,
     cells_ref, observed_ref, variance_ref, out_ref, sums_ref,
-    below_ref, above_ref, below_c, above_c, hot_ref, parts_ref, outgoing, incoming,
-    up_send, up_recv, down_send, down_recv, mem_send, mem_recv,
+    near_ref, far_ref, near_c, far_c, hot_ref, parts_ref, outgoing, incoming,
+    near_send, near_recv, far_send, far_recv, mem_send, mem_recv,
 ):
     tile, me = lax.axis_index("tile"), lax.axis_index("mem")
     members, height, width = prior_ref.shape
     group_columns = out_ref.shape[1]
     has_below, has_above = tile > 0, tile < tiles - 1
-    enter(tile, tiles, me, groups)
-
-    def halo(target, field, coefs, send, recv):
-        pairs = [(prior_ref, field)] + [
-            (ref, coefs.at[i]) for i, ref in enumerate((vy_ref, vx_ref, dk_ref))
-        ]
+    odd = lax.rem(tile, 2)
+    even = odd == 0
+    partner = tile + 1 - 2 * odd
+    onward = tile + 2 - 4 * odd
+    behind = tile - 2 + 4 * odd
+    passes = jnp.logical_and(onward >= 0, onward < tiles)
+    has_far = jnp.logical_and(behind >= 0, behind < tiles)
+    enter(tile, tiles, me, groups, (1 - 2 * odd, -2, 2))
+    chunk = members // CHUNKS
+
+    def hop(pairs, send, recv, target):
         return [
             pltpu.make_async_remote_copy(
                 src_ref=src, dst_ref=dst, send_sem=send.at[i], recv_sem=recv.at[i],
@@ -126,54 +133,55 @@
             for i, (src, dst) in enumerate(pairs)
         ]
 
-    up = halo(tile + 1, below_ref, below_c, up_send, up_recv)
-    down = halo(tile - 1, above_ref, above_c, down_send, down_recv)
-
-    @pl.when(has_above)
-    def _():
-        for c in up:
-            c.start()
-
-    @pl.when(has_below)
-    def _():
-        for c in down:
-            c.start()
-
-    @pl.when(jnp.logical_not(has_below))
-    def _():
-        below_ref[...] = jnp.zeros_like(below_ref)
-        below_c[...] = jnp.zeros_like(below_c)
-
-    @pl.when(jnp.logical_not(has_above))
-    def _():
-        above_ref[...] = jnp.zeros_like(above_ref)
-        above_c[...] = jnp.zeros_like(above_c)
-
-    build_hot(order_ref, hot_ref)
+    cuts = [pl.ds(i * chunk, chunk) for i in range(CHUNKS)]
+    first_hop = hop(
+        [(prior_ref.at[cut], near_ref.at[cut]) for cut in cuts]
+        + [(ref, near_c.at[i]) for i, ref in enumerate((vy_ref, vx_ref, dk_ref))],
+        near_send, near_recv, partner,
+    )
+    second_hop = hop(
+        [(near_ref.at[cut], far_ref.at[cut]) for cut in cuts]
+        + [(near_c.at[i], far_c.at[i]) for i in range(3)],
+        far_send, far_recv, onward,
+    )
+    for c in first_hop:
+        c.start()
+
+    @pl.when(jnp.logical_not(has_far))
+    def _():
+        far_ref[...] = jnp.zeros_like(far_ref)
+        far_c[...] = jnp.zeros_like(far_c)
+
+    for i in range(CHUNKS + 3):
+        if i < CHUNKS:
+            build_hot(order_ref, hot_ref, i, CHUNKS)
+        first_hop[i].wait_recv()
+
+        @pl.when(passes)
+        def _():
+            second_hop[i].start()
+
     observation_sums(cells_ref, observed_ref, variance_ref, sums_ref)
 
-    @pl.when(has_below)
-    def _():
-        for c in up:
-            c.wait_recv()
-
-    @pl.when(has_above)
-    def _():
-        for c in down:
+    @pl.when(has_far)
+    def _():
+        for c in second_hop:
             c.wait_recv()
 
     def slab(r):
         if r < 0:
-            return below_ref[:, height + r, :]
+            return jnp.where(even, far_ref[:, height + r, :], near_ref[:, height + r, :])
         if r >= height:
-            return above_ref[:, r - height, :]
+            return jnp.where(even, near_ref[:, r - height, :], far_ref[:, r - height, :])
         return prior_ref[:, r, :]
 
     def coefs(r):
         if r < 0:
-            return [below_c[i, height + r : height + r + 1, :] for i in range(3)]
+            at = slice(height + r, height + r + 1)
+            return [jnp.where(even, far_c[i, at, :], near_c[i, at, :]) for i in range(3)]
         if r >= height:
-            return [above_c[i, r - height : r - height + 1, :] for i in range(3)]
+            at = slice(r - height, r - height + 1)
+            return [jnp.where(even, near_c[i, at, :], far_c[i, at, :]) for i in range(3)]
         return [ref[r : r + 1, :] for ref in (vy_ref, vx_ref, dk_ref)]
 
     keep_below = jnp.where(has_below, 1.0, 0.0)
@@ -214,14 +222,12 @@
     for k, c in sent:
         c.wait_send()
 
-    @pl.when(has_above)
-    def _():
-        for c in up:
-            c.wait_send()
-
-    @pl.when(has_below)
-    def _():
-        for c in down:
+    for c in first_hop:
+        c.wait_send()
+
+    @pl.when(passes)
+    def _():
+        for c in second_hop:
             c.wait_send()
 
 
@@ -235,7 +241,7 @@
     height = extent - 4
     group_columns = updated_ref.shape[1]
     has_below, has_above = tile > 0, tile < tiles - 1
-    enter(tile, tiles, me, groups)
+    enter(tile, tiles, me, groups, (-1, 1))
     sent = []
     for k in sorted(range(1, groups), key=lambda k: abs(2 * k - groups)):
         target = lax.rem(me + k, groups)
@@ -435,7 +441,7 @@
             pltpu.VMEM((2 * members, columns), bf16),
             pltpu.VMEM((groups - 1, members, group_columns), f32),
             pltpu.VMEM((groups - 1, members, group_columns), f32),
-            dma((4,)), dma((4,)), dma((4,)), dma((4,)), dma((groups - 1,)), dma((groups - 1,)),
+            *[dma((CHUNKS + 3,))] * 4, dma((groups - 1,)), dma((groups - 1,)),
         ],
         compiler_params=pltpu.CompilerParams(collective_id=0, has_side_effects=True),
     )(prior_ensemble_fields, vel_y, vel_x, diffus, assign, obs_cell, obs_value, obs_var)

time: 49.3 us -> 46.3 us (0.939)
  Pallas kernels: 48.8 us -> 46 us
    pallas_call x1, Pallas kernels: 23.8 us -> 20.1 us  [on_device(): pl.pallas_call(functools.partial(forecast_kernel, tiles, groups), out_sha...]
    pallas_call x1, Pallas kernels: 16.5 us -> 17.4 us  [on_device(): pl.pallas_call(functools.partial(return_kernel, tiles, groups), out_shape...]
where the time goes in v4:
time: 46.3 us; the launch traced here: 46.1 us
  Pallas kernels  46 us (99%)
    pallas_call x1, Pallas kernels, on_device(): pl.pallas_call(functools.partial(forecast_kernel, tiles, groups), out_sha...  20.1 us
    pallas_call x1, Pallas kernels, on_device(): pl.pallas_call(functools.partial(return_kernel, tiles, groups), out_shape...  17.4 us
    pallas_call x1, Pallas kernels, analyze(): pl.pallas_call(analysis_kernel, out_shape=jax.ShapeDtypeStruct(members.sh...  6.38 us
    pallas_call x1, Pallas kernels, on_device(): pl.pallas_call(last_kernel, out_shape=jax.ShapeDtypeStruct((members, heig...  2.16 us

profile of v4, /device:TPU:16, one launch (start us, length us, event | category | flops | bytes accessed | tf_op | source)
XLA Modules:
  0.0 46.1 jit_solution(5039666273555144371)
XLA Ops:
  0.0 20.1 %shard_map.82 = (f32[128,512]{1,0:T(8,128)}, f32[16,256]{1,0:T(8,128)}) custom-call(f32[32,4,512]{2,1,0:T(4,128)} %prior_ref.1, f32[4,512]{1,0:T(4,128)} %vy_ref.3, f32[4,512]{1,0:T(4,128)} %vx_ref.3, f32[4,512]{1,0:T(4,128)} %dk_ref.3, s32[1,2048]{1,0:T(1,128)} %order_ref.3, s32[2,512]{1,0:T(2,128)} %cells_ref.1, f32[2,512]{1,0:T(2,128)} %observed_ref.1, ...), custom_call_target="tpu_custom_call" | custom-call | tf_op jit(solution)/shard_map/pallas_call | solution.py:427
  20.1 6.4 %shard_map.83.updated_ref = f32[128,512]{1,0:T(8,128)} custom-call(f32[128,512]{1,0:T(8,128)} %get-tuple-element.7.members_ref, f32[16,256]{1,0:T(8,128)} %get-tuple-element.8.sums_ref), custom_call_target="tpu_custom_call" | custom-call | tf_op jit(solution)/shard_map/pallas_call | solution.py:406
  26.5 17.4 %shard_map.84.rows_ref = f32[8,32,512]{2,1,0:T(8,128)} custom-call(f32[128,512]{1,0:T(8,128)} %shard_map.83.updated_ref, s32[1,2048]{1,0:T(1,128)} %order_ref.3), custom_call_target="tpu_custom_call" | custom-call | tf_op jit(solution)/shard_map/pallas_call | solution.py:449
  43.9 2.2 %shard_map.85 = f32[32,4,512]{2,1,0:T(4,128)} custom-call(f32[8,32,512]{2,1,0:T(8,128)} %shard_map.84.rows_ref, f32[4,512]{1,0:T(4,128)} %vy_ref.3, f32[4,512]{1,0:T(4,128)} %vx_ref.3, f32[4,512]{1,0:T(4,128)} %dk_ref.3), custom_call_target="tpu_custom_call" | custom-call | tf_op jit(solution)/shard_map/pallas_call | solution.py:464

commit v5 on v4

--- a/solution.py
+++ b/solution.py
@@ -10,7 +10,7 @@
 PATCH = 256
 
 
-CHUNKS = 4
+CHUNKS = 8
 MESH = pl.DeviceIdType.MESH
 NN = (((1,), (0,)), ((), ()))
 

time: 46.3 us -> 46 us (level); the launches traced: 46.1 us -> 45.2 us
  Pallas kernels: 46 us -> 45.2 us
    pallas_call x1, Pallas kernels: 20.1 us -> 19.6 us  [on_device(): pl.pallas_call(functools.partial(forecast_kernel, tiles, groups), out_sha...]
where the time goes in v5:
time: 46 us; the launch traced here: 45.2 us
  Pallas kernels  45.2 us (98%)
    pallas_call x1, Pallas kernels, on_device(): pl.pallas_call(functools.partial(forecast_kernel, tiles, groups), out_sha...  19.6 us
    pallas_call x1, Pallas kernels, on_device(): pl.pallas_call(functools.partial(return_kernel, tiles, groups), out_shape...  17 us
    pallas_call x1, Pallas kernels, analyze(): pl.pallas_call(analysis_kernel, out_shape=jax.ShapeDtypeStruct(members.sh...  6.38 us
    pallas_call x1, Pallas kernels, on_device(): pl.pallas_call(last_kernel, out_shape=jax.ShapeDtypeStruct((members, heig...  2.16 us

profile of v5, /device:TPU:16, one launch (start us, length us, event | category | flops | bytes accessed | tf_op | source)
XLA Modules:
  0.0 45.2 jit_solution(8567249886945671821)
XLA Ops:
  0.0 19.6 %shard_map.82 = (f32[128,512]{1,0:T(8,128)}, f32[16,256]{1,0:T(8,128)}) custom-call(f32[32,4,512]{2,1,0:T(4,128)} %prior_ref.1, f32[4,512]{1,0:T(4,128)} %vy_ref.3, f32[4,512]{1,0:T(4,128)} %vx_ref.3, f32[4,512]{1,0:T(4,128)} %dk_ref.3, s32[1,2048]{1,0:T(1,128)} %order_ref.3, s32[2,512]{1,0:T(2,128)} %cells_ref.1, f32[2,512]{1,0:T(2,128)} %observed_ref.1, ...), custom_call_target="tpu_custom_call" | custom-call | tf_op jit(solution)/shard_map/pallas_call | solution.py:427
  19.6 6.4 %shard_map.83.updated_ref = f32[128,512]{1,0:T(8,128)} custom-call(f32[128,512]{1,0:T(8,128)} %get-tuple-element.7.members_ref, f32[16,256]{1,0:T(8,128)} %get-tuple-element.8.sums_ref), custom_call_target="tpu_custom_call" | custom-call | tf_op jit(solution)/shard_map/pallas_call | solution.py:406
  26.0 17.0 %shard_map.84.rows_ref = f32[8,32,512]{2,1,0:T(8,128)} custom-call(f32[128,512]{1,0:T(8,128)} %shard_map.83.updated_ref, s32[1,2048]{1,0:T(1,128)} %order_ref.3), custom_call_target="tpu_custom_call" | custom-call | tf_op jit(solution)/shard_map/pallas_call | solution.py:449
  43.0 2.2 %shard_map.85 = f32[32,4,512]{2,1,0:T(4,128)} custom-call(f32[8,32,512]{2,1,0:T(8,128)} %shard_map.84.rows_ref, f32[4,512]{1,0:T(4,128)} %vy_ref.3, f32[4,512]{1,0:T(4,128)} %vx_ref.3, f32[4,512]{1,0:T(4,128)} %dk_ref.3), custom_call_target="tpu_custom_call" | custom-call | tf_op jit(solution)/shard_map/pallas_call | solution.py:464
